TPU v7x, 256 devices: a whole 4x4x8 slice. The times are simulated.
256 devices in a mesh: row: 8 (over x, core), col: 16 (over y_lo, z), kern: 2 (over y_hi).
Axes of the slice: x: 4, y: 4 (y_hi: 2, y_lo: 2; y = y_hi * 2 + y_lo), z: 8, core: 2. Of those that a mesh axis runs over, the one named last changes fastest.
Arguments:
- mask_levels: int32 [256, 8192], P('row', 'col'), may hold values from 0 to 3
- level_offset: float32 [256, 8192], P('row', 'col'), may hold values from -6 to 6
- target_bits: int32 [256, 8192], P('row', 'col'), may hold values 0 or 1
- socs_kernels: bfloat16 [2, 24, 35, 35], P(None, 'kern'), may hold values from -0.067871094 to 0.067871094
- kernel_weights: float32 [24], P('kern'), may hold values from 0.1 to 1
Outputs:
- resist_image: float32 [256, 8192], P('row', 'col')
- mask_gradient: float32 [256, 8192], P('row', 'col')
All inputs are finite; a program needn't handle non-finite values. No bound on the sum of `target_bits` on one device may be relied on, other than what follows from the above.
Results may differ from a plain program's by a relative error of at most 0.0039.
Values may be sent and summed in bfloat16 or wider, within the bound.
No kernel may reach another device: no remote copies, remote signals or barrier semaphores. Data moves between devices by JAX's collectives and lax.ppermute only.
A program may use at most 64 MiB of HBM per device.

v0:
```python
import jax
import jax.numpy as jnp
from jax import lax
from jax.sharding import PartitionSpec as P

steepness = 4.0
threshold = 1.0
loss_gain = 32.0


def padded_2(value, sides, width):
    for axis, dim in sides:
        size, length = (lax.axis_size(axis), value.shape[dim])
        up = [(i, (i + 1) % size) for i in range(size - 1)]
        down = [(j, i) for i, j in up]
        last = lax.slice_in_dim(value, length - width, length, axis=dim)
        first = lax.slice_in_dim(value, 0, width, axis=dim)
        before = lax.ppermute(last, axis, up)
        after = lax.ppermute(first, axis, down)
        value = jnp.concatenate([before, value, after], axis=dim)
    return value


def column_windows(padded, blocks, reach):
    leading = padded.shape[:-1]
    central = padded[..., : blocks * 128].reshape(leading + (blocks, 128))
    filler = jnp.zeros(leading + (128 - reach,), padded.dtype)
    longer = jnp.concatenate([padded, filler], axis=-1)
    trailing = longer[..., 128:].reshape(leading + (blocks, 128))[..., :reach]
    return jnp.concatenate([central, trailing], axis=-1)


def band_select(stencil):
    window = 128 + stencil - 1
    offsets = (
        jnp.arange(window, dtype=jnp.int32)[:, None, None]
        - jnp.arange(128, dtype=jnp.int32)[None, :, None]
    )
    return (offsets == jnp.arange(stencil, dtype=jnp.int32)[None, None, :]).astype(jnp.bfloat16)


def forward_row(select, kernels, tap_row):
    kernel_row = lax.dynamic_index_in_dim(kernels, tap_row, 2, keepdims=False)
    toeplitz = jnp.einsum("job,ckb->jcko", select, kernel_row, preferred_element_type=jnp.float32)
    return toeplitz.astype(jnp.bfloat16).reshape(select.shape[0], -1)


def adjoint_row(select, flipped, tap_row):
    kernel_row = lax.dynamic_index_in_dim(flipped, tap_row, 2, keepdims=False)
    toeplitz = jnp.einsum("job,ckb->ckjo", select, kernel_row, preferred_element_type=jnp.float32)
    return toeplitz.astype(jnp.bfloat16).reshape(2 * flipped.shape[1], select.shape[0], 128)


def resist_terms(intensity, target):
    resist = jax.nn.sigmoid(steepness * (intensity - threshold))
    slope_term = (
        loss_gain * steepness * (resist - target.astype(jnp.float32)) * resist * (1.0 - resist)
    )
    return (resist, slope_term)


def per_device(mask_levels, level_offset, target_bits, socs_kernels, kernel_weights):
    tile_rows, tile_cols = mask_levels.shape
    stencil = socs_kernels.shape[-1]
    margin = stencil // 2
    reach = 2 * margin
    blocks = tile_cols // 128
    local_kernels = socs_kernels.shape[1]
    channels = 2 * local_kernels
    select = band_select(stencil)
    flipped = socs_kernels[:, :, ::-1, ::-1]
    mask_full = jax.nn.sigmoid(2.0 * (mask_levels.astype(jnp.float32) - 1.5) + level_offset)
    mask_bf = mask_full.astype(jnp.bfloat16)
    padded = padded_2(mask_bf, (("row", 0), ("col", 1)), margin)
    windows = column_windows(padded, blocks, reach)

    def forward_step(tap_row, running):
        row_slab = lax.dynamic_slice_in_dim(windows, tap_row, tile_rows, 0)
        weights_row = forward_row(select, socs_kernels, tap_row)
        return running + jnp.einsum(
            "xnj,jf->xnf", row_slab, weights_row, preferred_element_type=jnp.float32
        )

    fields = lax.fori_loop(
        0, stencil, forward_step, jnp.zeros((tile_rows, blocks, channels * 128), jnp.float32)
    )
    fields = fields.reshape(tile_rows, blocks, 2, local_kernels, 128)
    partial_value = jnp.sum(
        fields * fields * kernel_weights[None, None, None, :, None], axis=(2, 3)
    )
    partial_value = partial_value.reshape(tile_rows, tile_cols)
    intensity = lax.psum(partial_value, "kern")
    resist, slope_term = resist_terms(intensity, target_bits)
    scaled = (
        2.0
        * kernel_weights[None, None, None, :, None]
        * slope_term.reshape(tile_rows, blocks, 1, 1, 128)
    )
    charge = (scaled * fields).astype(jnp.bfloat16)
    charge = jnp.transpose(charge, (2, 3, 0, 1, 4)).reshape(channels, tile_rows, tile_cols)
    charge_padded = padded_2(charge, (("row", 1), ("col", 2)), margin)
    charge_windows = column_windows(charge_padded, blocks, reach)

    def adjoint_step(tap_row, running):
        row_slab = lax.dynamic_slice_in_dim(charge_windows, tap_row, tile_rows, 1)
        weights_row = adjoint_row(select, flipped, tap_row)
        return running + jnp.einsum(
            "cxnj,cjo->xno", row_slab, weights_row, preferred_element_type=jnp.float32
        )

    gradient_part = lax.fori_loop(
        0, stencil, adjoint_step, jnp.zeros((tile_rows, blocks, 128), jnp.float32)
    )
    gradient_part = gradient_part.reshape(tile_rows, tile_cols)
    summed = lax.psum(gradient_part, "kern")
    return (resist, summed * mask_full * (1.0 - mask_full))


def solution(mesh):
    return jax.shard_map(
        per_device,
        mesh=mesh,
        in_specs=(
            P("row", "col"),
            P("row", "col"),
            P("row", "col"),
            P(None, "kern", None, None),
            P("kern"),
        ),
        out_specs=(P("row", "col"), P("row", "col")),
        check_vma=False,
    )
```

profile of v0, /device:TPU:10, one launch (start us, length us, event | category | flops | bytes accessed | tf_op | source)
XLA Modules:
  0.0 471.2 jit_solution(10960512505497129558)
XLA Ops:
  10.1 3.6 collective-permute-start.1
  15.3 3.8 collective-permute-start.2
  19.1 5.7 %collective-permute-start.3 = (bf16[66,17]{1,0:T(8,128)(2,1)S(1)}, bf16[66,17]{1,0:T(8,128)(2,1)S(1)}, u32[]{:S(2)}, u32[]{:S(2)}) collective-permute-start(bf16[66,17]{1,0:T(8,128)(2,1)S(1)} %get-tuple-element.300), channel_id=1, source_target_pairs={{2,0},{4,2},{6,4},{8,6},{10,8},{12,10},{14,12},{16,14},{18,16},{20... | collective-permute-start | bytes 6740 | tf_op jit(solution)/shard_map/ppermute | solution.py:19
  26.6 157.3 %while.28 = (s32[]{:T(128)}, f32[32,4,3072]{2,0,1:T(8,128)}, bf16[66,4,162]{2,0,1:T(8,128)(2,1)S(1)}, bf16[2,12,35,35]{3,1,0,2:T(8,128)(2,1)S(1)}, s32[162,128]{1,0:T(8,128)S(1)}, /*index=5*/s32[]{:T(128)}, s32[]{:T(128)}) while((s32[]{:T(128)}, f32[32,4,3072]{2,0,1:T(8,128)}, bf16[66,4,162]{2,0,1:T(8,128)(2,1)S(1)}, ...), condition=%wide.region_1.2_spmd.clone, body=%wide.region_0.1_spmd.clone.sunk | while | flops 164974080 | bytes 9314399 | solution.py:84
  63.0 3.0 convolution_add_fusion.2
  67.5 3.0 convolution_add_fusion.2
  72.0 3.0 convolution_add_fusion.2
  81.1 3.0 convolution_add_fusion.2
  90.2 3.0 convolution_add_fusion.2
  103.8 3.0 convolution_add_fusion.2
  112.9 3.0 convolution_add_fusion.2
  121.9 3.0 convolution_add_fusion.2
  131.0 3.0 convolution_add_fusion.2
  187.0 34.5 %all-reduce.3.cloned.1.call-done = f32[32,512]{1,0:T(8,128)} async-done(((f32[32,512]{1,0:T(8,128)}), f32[32,512]{1,0:T(8,128)}) %all-reduce.3.cloned.1.call-update) | async-done | bytes 65552 | tf_op jit(solution)/shard_map/psum | solution.py:92
  227.0 3.6 collective-permute-start.5
  230.7 3.6 collective-permute-done.4
  237.4 3.4 collective-permute-start.6
  240.8 4.7 %collective-permute-start.7 = (bf16[24,66,17]{2,1,0:T(8,128)(2,1)S(1)}, bf16[24,66,17]{2,1,0:T(8,128)(2,1)}, u32[]{:S(2)}, u32[]{:S(2)}) collective-permute-start(bf16[24,66,17]{2,1,0:T(8,128)(2,1)S(1)} %get-tuple-element.294), channel_id=1, source_target_pairs={{2,0},{4,2},{6,4},{8,6},{10,8},{12,10},{14,12},{16,14},{18,16},{20... | collective-permute-start | bytes 161576 | tf_op jit(solution)/shard_map/ppermute | solution.py:19
  246.5 7.1 %collective-permute-done.6 = bf16[24,66,17]{2,1,0:T(8,128)(2,1)S(1)} collective-permute-done((bf16[24,66,17]{2,1,0:T(8,128)(2,1)}, bf16[24,66,17]{2,1,0:T(8,128)(2,1)S(1)}, u32[]{:S(2)}, u32[]{:S(2)}) %collective-permute-start.6) | collective-permute-done | bytes 53888 | tf_op jit(solution)/shard_map/ppermute | solution.py:18
  255.5 6.0 %pad_maximum_fusion.4 = (bf16[24,66,512]{2,1,0:T(8,128)(2,1)S(1)}, bf16[24,66,512]{2,1,0:T(8,128)(2,1)}) fusion(bf16[24,66,17]{2,1,0:T(8,128)(2,1)} %copy-done.1, bf16[24,17,512]{2,1,0:T(8,128)(2,1)} %copy-done, bf16[24,32,512]{2,1,0:T(8,128)(2,1)S(1)} %reshape.72, bf16[24,17,512]{2,1,0:T(8,128)(2,1)S(1)} %copy.51, bf16[512]{0:T(512)(128)(2,1)S(1)} %pad_slice_fusion, ...), kind=kLoop, calls=%fused_computation.36 | loop fusion | flops 14598144 | bytes 4974784 | tf_op jit(solution)/shard_map/concatenate | solution.py:20
  261.5 3.7 reshape.86
  267.2 5.5 %pad_maximum_fusion = bf16[24,66,4,162]{3,2,1,0:T(4,128)(2,1)} fusion(bf16[24,66,4,34]{3,2,1,0:T(4,128)(2,1)} %bitcast.76, bf16[24,66,4,128]{3,2,1,0:T(4,128)(2,1)} %reshape.85), kind=kLoop, calls=%fused_computation.29 | loop fusion | flops 4105728 | bytes 4105728 | tf_op jit(solution)/shard_map/concatenate | solution.py:30
  272.7 155.4 %while.29 = (s32[]{:T(128)}, f32[32,4,128]{2,0,1:T(8,128)S(1)}, bf16[24,66,4,162]{3,2,1,0:T(4,128)(2,1)}, bf16[2,12,35,35]{3,1,0,2:T(8,128)(2,1)}, s32[162,128]{1,0:T(8,128)S(1)}, /*index=5*/s32[]{:T(128)}, s32[]{:T(128)}) while((s32[]{:T(128)}, f32[32,4,128]{2,0,1:T(8,128)S(1)}, bf16[24,66,4,162]{3,2,1,0:T(4,128)(2,1)}, ...), condition=%wide.region_5.6_spmd.clone, body=%wide.region_4.5_spmd.clone.sunk | while | flops 164220416 | bytes 7190107 | solution.py:111
  428.8 34.0 %all-reduce.5.cloned.1.call-done = f32[32,512]{1,0:T(8,128)} async-done(((f32[32,512]{1,0:T(8,128)}), f32[32,512]{1,0:T(8,128)}) %all-reduce.5.cloned.1.call-update) | async-done | bytes 65552 | tf_op jit(solution)/shard_map/psum | solution.py:115
  (330 shorter events, 307.7 us)
Async XLA Ops:
  7.2 214.3 %all-reduce.3.cloned.1.call-start = ((), (), s32[]{:S(2)}) async-start(), calls=%async_computation | async-start | bytes 131072 | tf_op jit(solution)/shard_map/psum | solution.py:92
  8.1 5.6 %collective-permute-start = (bf16[17,512]{1,0:T(8,128)(2,1)S(1)}, bf16[17,512]{1,0:T(8,128)(2,1)S(1)}, u32[]{:S(2)}, u32[]{:S(2)}) collective-permute-start(bf16[17,512]{1,0:T(8,128)(2,1)S(1)} %get-tuple-element.301), channel_id=1, source_target_pairs={{0,32},{32,64},{64,96},{96,128},{128,160},{160,192},{192,224},{1,3... | collective-permute-start | bytes 52232 | tf_op jit(solution)/shard_map/ppermute | solution.py:18
  10.1 5.1 %collective-permute-start.1 = (bf16[17,512]{1,0:T(8,128)(2,1)S(1)}, bf16[17,512]{1,0:T(8,128)(2,1)S(1)}, u32[]{:S(2)}, u32[]{:S(2)}) collective-permute-start(bf16[17,512]{1,0:T(8,128)(2,1)S(1)} %get-tuple-element.302), channel_id=1, source_target_pairs={{32,0},{64,32},{96,64},{128,96},{160,128},{192,160},{224,192},{33,... | collective-permute-start | bytes 52232 | tf_op jit(solution)/shard_map/ppermute | solution.py:19
  15.3 10.7 %collective-permute-start.2 = (bf16[66,17]{1,0:T(8,128)(2,1)S(1)}, bf16[66,17]{1,0:T(8,128)(2,1)S(1)}, u32[]{:S(2)}, u32[]{:S(2)}) collective-permute-start(bf16[66,17]{1,0:T(8,128)(2,1)S(1)} %get-tuple-element.299), channel_id=1, source_target_pairs={{0,2},{2,4},{4,6},{6,8},{8,10},{10,12},{12,14},{14,16},{16,18},{18... | collective-permute-start | bytes 6740 | tf_op jit(solution)/shard_map/ppermute | solution.py:18
  19.1 7.2 %collective-permute-start.3 = (bf16[66,17]{1,0:T(8,128)(2,1)S(1)}, bf16[66,17]{1,0:T(8,128)(2,1)S(1)}, u32[]{:S(2)}, u32[]{:S(2)}) collective-permute-start(bf16[66,17]{1,0:T(8,128)(2,1)S(1)} %get-tuple-element.300), channel_id=1, source_target_pairs={{2,0},{4,2},{6,4},{8,6},{10,8},{12,10},{14,12},{16,14},{18,16},{20... | collective-permute-start | bytes 6740 | tf_op jit(solution)/shard_map/ppermute | solution.py:19
  183.9 1.7 copy-start.5
  185.6 35.9 %copy-start.4 = (s32[32,512]{1,0:T(8,128)S(1)}, s32[32,512]{1,0:T(8,128)}, u32[]{:S(2)}) copy-start(s32[32,512]{1,0:T(8,128)} %param.11) | copy-start | bytes 196612
  186.9 276.0 %all-reduce.5.cloned.1.call-start = ((), (), s32[]{:S(2)}) async-start(), calls=%async_computation.1 | async-start | bytes 131072 | tf_op jit(solution)/shard_map/psum | solution.py:115
  225.0 9.4 %collective-permute-start.4 = (bf16[24,17,512]{2,0,1:T(8,128)(2,1)S(1)}, bf16[24,17,512]{2,0,1:T(8,128)(2,1)S(1)}, u32[]{:S(2)}, u32[]{:S(2)}) collective-permute-start(bf16[24,17,512]{2,0,1:T(8,128)(2,1)S(1)} %copy.49), channel_id=1, source_target_pairs={{0,32},{32,64},{64,96},{96,128},{128,160},{160,192},{192,224},{1,3... | collective-permute-start | bytes 1253384 | tf_op jit(solution)/shard_map/ppermute | solution.py:18
  227.0 9.2 %collective-permute-start.5 = (bf16[24,17,512]{2,0,1:T(8,128)(2,1)S(1)}, bf16[24,17,512]{2,0,1:T(8,128)(2,1)S(1)}, u32[]{:S(2)}, u32[]{:S(2)}) collective-permute-start(bf16[24,17,512]{2,0,1:T(8,128)(2,1)S(1)} %copy.50), channel_id=1, source_target_pairs={{32,0},{64,32},{96,64},{128,96},{160,128},{192,160},{224,192},{33,... | collective-permute-start | bytes 1253384 | tf_op jit(solution)/shard_map/ppermute | solution.py:19
  236.4 17.3 %copy-start = (bf16[24,17,512]{2,1,0:T(8,128)(2,1)}, bf16[24,17,512]{2,1,0:T(8,128)(2,1)S(1)}, u32[]{:S(2)}) copy-start(bf16[24,17,512]{2,1,0:T(8,128)(2,1)S(1)} %copy.52) | copy-start | bytes 1253380
  237.4 16.2 %collective-permute-start.6 = (bf16[24,66,17]{2,1,0:T(8,128)(2,1)}, bf16[24,66,17]{2,1,0:T(8,128)(2,1)S(1)}, u32[]{:S(2)}, u32[]{:S(2)}) collective-permute-start(bf16[24,66,17]{2,1,0:T(8,128)(2,1)} %get-tuple-element.293), channel_id=1, source_target_pairs={{0,2},{2,4},{4,6},{6,8},{8,10},{10,12},{12,14},{14,16},{16,18},{18... | collective-permute-start | bytes 161576 | tf_op jit(solution)/shard_map/ppermute | solution.py:18
  240.8 14.6 %collective-permute-start.7 = (bf16[24,66,17]{2,1,0:T(8,128)(2,1)S(1)}, bf16[24,66,17]{2,1,0:T(8,128)(2,1)}, u32[]{:S(2)}, u32[]{:S(2)}) collective-permute-start(bf16[24,66,17]{2,1,0:T(8,128)(2,1)S(1)} %get-tuple-element.294), channel_id=1, source_target_pairs={{2,0},{4,2},{6,4},{8,6},{10,8},{12,10},{14,12},{16,14},{18,16},{20... | collective-permute-start | bytes 161576 | tf_op jit(solution)/shard_map/ppermute | solution.py:19
  253.6 0.8 copy-start.1
  272.7 190.1 %copy-start.2 = (f32[32,512]{1,0:T(8,128)S(1)}, f32[32,512]{1,0:T(8,128)}, u32[]{:S(2)}) copy-start(f32[32,512]{1,0:T(8,128)} %param.10) | copy-start | bytes 196612
  272.7 190.1 %copy-start.3 = (s32[32,512]{1,0:T(8,128)S(1)}, s32[32,512]{1,0:T(8,128)}, u32[]{:S(2)}) copy-start(s32[32,512]{1,0:T(8,128)} %param.9) | copy-start | bytes 196612
Sparse Core Ops, SparseCore 0:
  187.0 34.4 all-reduce.2
  429.0 33.8 all-reduce.4
where the time goes:
time: 477 us; the launch traced here: 471 us
  matrix products  192 us (40%)
  local copies, waits for them, and re-layouts  132 us (28%)
  waiting for transfers between devices  84 us (18%)
  starting transfers between devices  29 us (6%)
  other arithmetic  18 us (4%)
  between operations  14.3 us (3%)
    dot_general x35, matrix products, forward_step(): jnp.einsum('xnj,jf->xnf', row_slab, weights_row, preferred_element_type=j...  103 us
    dynamic_slice x35, local copies, waits for them, and re-layouts, adjoint_step(): row_slab = lax.dynamic_slice_in_dim(charge_windows, tap_row, tile_rows, 1)  77.8 us
    dot_general x35, matrix products, adjoint_row(): jnp.einsum('job,ckb->ckjo', select, kernel_row, preferred_element_type=jn...  46.3 us
    psum x1, waiting for transfers between devices, per_device(): intensity = lax.psum(partial_value, 'kern')  34.5 us
    psum x1, waiting for transfers between devices, per_device(): summed = lax.psum(gradient_part, 'kern')  34 us
    reshape x35, local copies, waits for them, and re-layouts, forward_row(): return toeplitz.astype(jnp.bfloat16).reshape(select.shape[0], -1)  23.3 us
    dot_general x35, matrix products, forward_row(): jnp.einsum('job,ckb->jcko', select, kernel_row, preferred_element_type=jn...  21.6 us
    dot_general x35, matrix products, adjoint_step(): jnp.einsum('cxnj,cjo->xno', row_slab, weights_row, preferred_element_type...  20.4 us
  transfers between devices with their start and end apart: 10, of which 8 were waited for; matrix products, arithmetic and copies ran while one was open for 0% of the time, Pallas kernels for 0%

commit v1 on v0

v1 whole, which is shorter than its diff:
```python
import jax
import jax.numpy as jnp
from jax import lax
from jax.experimental import pallas as pl
from jax.experimental.pallas import tpu as pltpu
from jax.sharding import PartitionSpec as P

STEEP = 4.0
THRESHOLD = 1.0
GAIN = 128.0
TAPS = 35
MARGIN = 17
SLOT = 40
BLOCK = 8
EDGE = 128
ROWS = 32
CHANNELS = 48
REACH = BLOCK + TAPS - 1
FWD_K = 1792
LEAD = 6
WIDE = 384
BF = jnp.bfloat16
F32 = jnp.float32


def body(top, own, bot, tgt, wgt, fwd, adj, res_out, up_out, mid_out, dn_out, rows, image, charge):
    rows[0:32, :] = top[...].astype(F32)
    rows[32:64, :] = own[...].astype(F32)
    rows[64:96, :] = bot[...].astype(F32)
    image[2640:2752, :] = jnp.zeros((112, WIDE), BF)

    def build(p, carry):
        parts = []
        for i in range(2):
            line = jnp.broadcast_to(rows[pl.ds(15 + 2 * p + i, 1), :], (SLOT, 512))
            parts.append(pltpu.roll(line, 0, 1, stride=1, stride_axis=0)[:, 128:])
        both = jnp.concatenate(parts, axis=0).astype(BF)
        image[pl.ds(pl.multiple_of(p * 80, 80), 80), :] = both
        return carry

    lax.fori_loop(0, 33, build, 0)
    weight = wgt[...]
    goal = pltpu.roll(tgt[...].astype(F32), 512 - 111, 1)[:, :WIDE]
    for j in range(4):
        fields = jnp.dot(fwd[...], image[320 * j : 320 * j + FWD_K, :], preferred_element_type=F32)
        fields = fields.reshape(BLOCK, CHANNELS, WIDE)
        intensity = jnp.sum(weight[None] * fields * fields, axis=1)
        resist = jax.nn.sigmoid(STEEP * (intensity - THRESHOLD))
        want = goal[8 * j : 8 * j + 8]
        slope = GAIN * (resist - want) * resist * (1.0 - resist)
        slope = jnp.where(want > 1.5, 0.0, slope)
        scaled = (2.0 * weight)[None] * slope[:, None, :] * fields
        charge[384 * j : 384 * j + 384, :] = scaled.astype(BF).reshape(BLOCK * CHANNELS, WIDE)
        res_out[8 * j : 8 * j + 8, :] = pltpu.roll(resist, WIDE - MARGIN, 1)[:, :256]
    up_out[...] = jnp.zeros((ROWS, 256), F32)
    dn_out[...] = jnp.zeros((ROWS, 256), F32)
    for j in range(9):
        low = max(0, 40 - 8 * j)
        high = min(48, 72 - 8 * j)
        first = low - 40 + 8 * j
        part = jnp.dot(
            adj[:, 48 * low : 48 * high],
            charge[48 * first : 48 * (first + high - low), :],
            preferred_element_type=F32,
        )
        for i in range(BLOCK):
            x = 8 * j + i - MARGIN
            if x > 48:
                continue
            moved = pltpu.roll(part[SLOT * i : SLOT * i + SLOT], 0, 1, stride=1, stride_axis=0)
            line = jnp.sum(moved, axis=0, keepdims=True)
            line = pltpu.roll(line, WIDE - 34, 1)[:, :256]
            if x < 0:
                up_out[ROWS + x : ROWS + x + 1, :] = line
            elif x < ROWS:
                mid_out[x : x + 1, :] = line
            else:
                dn_out[x - ROWS : x - ROWS + 1, :] = line


def per_device(mask_levels, level_offset, target_bits, socs_kernels, kernel_weights):
    kern = lax.axis_index("kern")
    col = lax.axis_index("col")
    n_row, n_col = lax.axis_size("row"), lax.axis_size("col")
    mask_full = jax.nn.sigmoid(2.0 * (mask_levels.astype(F32) - 1.5) + level_offset)
    mask_bf = mask_full.astype(BF)
    target = target_bits.astype(BF)
    left = kern == 0

    strips = jnp.concatenate(
        [
            jnp.where(left, mask_bf[:, :EDGE], mask_bf[:, -EDGE:]),
            jnp.where(left, target[:, :EDGE], target[:, -EDGE:]),
        ],
        axis=0,
    )
    groups = socs_kernels.reshape(8, 3, TAPS, TAPS)
    groups = jnp.pad(groups, ((0, 0), (0, 0), (0, 5), (0, 5)))
    packed = jnp.concatenate([groups[:, 0], groups[:, 1], groups[:, 2]], axis=-1)
    packed = jnp.pad(packed, ((0, 0), (0, 0), (0, 8))).reshape(320, 128)
    high = lax.reduce_precision(kernel_weights, 8, 7)
    middle = lax.reduce_precision(kernel_weights - high, 8, 7)
    lower = kernel_weights - high - middle
    parts = jnp.pad(jnp.stack([high, middle, lower]).astype(BF), ((0, 5), (0, 116)))
    payload = jnp.concatenate([strips, packed, parts], axis=0)
    pairs = []
    for c in range(n_col):
        a, b = (2 * c + 1, 2 * ((c + 1) % n_col))
        pairs += [(a, b), (b, a)]
    other = lax.ppermute(payload, ("col", "kern"), pairs)
    outside = jnp.where(left, col == 0, col == n_col - 1)
    strip_mask = jnp.where(outside, jnp.zeros((), BF), other[:32])
    strip_target = jnp.where(outside, jnp.full((), 2.0, BF), other[32:64])

    def window(value, strip):
        return jnp.where(
            left,
            jnp.concatenate([strip, value[:, :384]], axis=1),
            jnp.concatenate([value[:, 128:], strip], axis=1),
        )

    own = window(mask_bf, strip_mask)
    goal = window(target, strip_target)
    down = [(i, i + 1) for i in range(n_row - 1)]
    upward = [(i + 1, i) for i in range(n_row - 1)]
    top = lax.ppermute(own, "row", down)
    bottom = lax.ppermute(own, "row", upward)

    got = other[64:384].reshape(8, 40, 128)
    got = jnp.stack([got[:, :35, 0:35], got[:, :35, 40:75], got[:, :35, 80:115]], axis=1)
    taps = jnp.concatenate([socs_kernels.reshape(24, TAPS, TAPS), got.reshape(24, TAPS, TAPS)], axis=0)
    far = other[384:387, :12].astype(F32)
    far = (far[0] + far[1]) + far[2]
    weights = jnp.concatenate([kernel_weights, kernel_weights, far, far])
    weights = jnp.broadcast_to(weights[:, None], (CHANNELS, WIDE))
    flat = jnp.pad(taps[:, :, ::-1], ((0, 0), (0, 0), (0, 5))).reshape(CHANNELS, TAPS * SLOT)
    fwd = jnp.concatenate(
        [jnp.pad(flat, ((0, 0), (SLOT * i, FWD_K - 1400 - SLOT * i))) for i in range(BLOCK)], axis=0
    )
    turned = jnp.transpose(taps[:, ::-1, :], (2, 1, 0)).reshape(TAPS, TAPS * CHANNELS)
    turned = jnp.pad(turned, ((0, 5), (0, 0)))
    adj = jnp.concatenate(
        [
            jnp.pad(turned, ((0, 0), (CHANNELS * (LEAD + i), CHANNELS * (48 - TAPS - LEAD - i))))
            for i in range(BLOCK)
        ],
        axis=0,
    )

    tile = jax.ShapeDtypeStruct((ROWS, 256), F32)
    vmem = pl.BlockSpec(memory_space=pltpu.VMEM)
    resist, up, middle_rows, dn = pl.pallas_call(
        body,
        out_shape=(tile,) * 4,
        in_specs=[vmem] * 7,
        out_specs=(vmem,) * 4,
        scratch_shapes=[
            pltpu.VMEM((96, 512), F32),
            pltpu.VMEM((2752, WIDE), BF),
            pltpu.VMEM((1536, WIDE), BF),
        ],
        compiler_params=pltpu.CompilerParams(vmem_limit_bytes=40 * 2**20),
    )(top, own, bottom, goal, weights, fwd, adj)
    from_below = lax.ppermute(up, "row", upward)
    from_above = lax.ppermute(dn, "row", down)
    half = jnp.where(left, mask_full[:, :256], mask_full[:, 256:])
    gradient = (middle_rows + from_below + from_above) * half * (1.0 - half)
    mine = jnp.concatenate([resist, gradient], axis=0)
    theirs = lax.ppermute(mine, "kern", [(0, 1), (1, 0)])
    both = jnp.where(
        left, jnp.concatenate([mine, theirs], axis=1), jnp.concatenate([theirs, mine], axis=1)
    )
    return both[:ROWS], both[ROWS:]


def solution(mesh):
    return jax.shard_map(
        per_device,
        mesh=mesh,
        in_specs=(
            P("row", "col"),
            P("row", "col"),
            P("row", "col"),
            P(None, "kern", None, None),
            P("kern"),
        ),
        out_specs=(P("row", "col"), P("row", "col")),
        check_vma=False,
    )
```

time: 477 us -> 51.4 us (0.11)
  the two profiles are of different devices: /device:TPU:10 before, /device:TPU:6 now
where the time goes in v1:
time: 51.4 us; the launch traced here: 51.1 us
  starting transfers between devices  18.4 us (36%)
  waiting for transfers between devices  11.7 us (23%)
  Pallas kernels  9.58 us (19%)
  local copies, waits for them, and re-layouts  7.56 us (15%)
  other arithmetic  2.9 us (6%)
  between operations  0.99 us (2%)
    pallas_call x1, Pallas kernels, per_device(): pl.pallas_call(body, out_shape=(tile,) * 4, in_specs=[vmem] * 7, out_spec...  9.58 us
    ppermute x1, starting transfers between devices, per_device(): other = lax.ppermute(payload, ('col', 'kern'), pairs)  8.39 us
    ppermute x1, waiting for transfers between devices, per_device(): theirs = lax.ppermute(mine, 'kern', [(0, 1), (1, 0)])  5.76 us
    ppermute x1, starting transfers between devices, per_device(): bottom = lax.ppermute(own, 'row', upward)  3.64 us
    ppermute x1, waiting for transfers between devices, per_device(): from_above = lax.ppermute(dn, 'row', down)  3.1 us
    ppermute x1, waiting for transfers between devices, per_device(): other = lax.ppermute(payload, ('col', 'kern'), pairs)  2.81 us
    unnamed x17, local copies, waits for them, and re-layouts  2.29 us
    ppermute x1, starting transfers between devices, per_device(): from_below = lax.ppermute(up, 'row', upward)  2.21 us
  transfers between devices with their start and end apart: 6, of which 3 were waited for; matrix products, arithmetic and copies ran while one was open for 6% of the time, Pallas kernels for 0%

profile of v1, /device:TPU:6, one launch (start us, length us, event | category | flops | bytes accessed | tf_op | source)
XLA Modules:
  0.0 51.1 jit_solution(4579508256695557867)
XLA Ops:
  0.6 0.8 %convert_element_type.57 = bf16[32,512]{1,0:T(8,128)(2,1)S(1)} convert(s32[32,512]{1,0:T(8,128)} %param.7) | non-fusion elementwise | flops 16384 | bytes 98304 | tf_op jit(solution)/shard_map/convert_element_type | solution.py:87
  1.5 1.0 %copy.9 = bf16[2,12,35,35]{3,2,1,0:T(8,128)(2,1)S(1)} copy(bf16[2,12,35,35]{3,0,2,1:T(2,128)(2,1)} %param.8) | data formatting | bytes 117600 | tf_op args[3]
  2.5 0.7 %fusion.17 = (bf16[1,12]{1,0:T(2,128)(2,1)S(1)}, bf16[1,12]{1,0:T(2,128)(2,1)S(1)}, bf16[1,12]{1,0:T(2,128)(2,1)S(1)}) fusion(f32[12]{0:T(128)} %param.9), kind=kLoop, calls=%fused_computation.61 | loop fusion | flops 84 | bytes 120 | tf_op jit(solution)/shard_map/stack | solution.py:104
  3.2 0.9 %fusion.21 = (bf16[32,512]{1,0:T(8,128)(2,1)S(1)}, f32[32,512]{1,0:T(8,128)S(1)}) fusion(f32[32,512]{1,0:T(8,128)} %param.6, s32[32,512]{1,0:T(8,128)} %param.5), kind=kLoop, calls=%fused_computation.67 | loop fusion | flops 131072 | bytes 229376 | tf_op jit(solution)/shard_map/convert_element_type | solution.py:86
  4.1 0.1 fusion.4
  4.3 8.4 %collective-permute-start = (bf16[392,128]{1,0:T(8,128)(2,1)S(1)}, bf16[392,128]{1,0:T(8,128)(2,1)S(1)}, u32[]{:S(2)}, u32[]{:S(2)}) collective-permute-start(bf16[392,128]{1,0:T(8,128)(2,1)S(1)} %pad_maximum_fusion.2), channel_id=1, source_target_pairs={{1,2},{2,1},{3,4},{4,3},{5,6},{6,5},{7,8},{8,7},{9,10},{10,9},{11,... | collective-permute-start | bytes 301064 | tf_op jit(solution)/shard_map/ppermute | solution.py:110
  12.7 2.8 %collective-permute-done = bf16[392,128]{1,0:T(8,128)(2,1)S(1)} collective-permute-done((bf16[392,128]{1,0:T(8,128)(2,1)S(1)}, bf16[392,128]{1,0:T(8,128)(2,1)S(1)}, u32[]{:S(2)}, u32[]{:S(2)}) %collective-permute-start) | collective-permute-done | bytes 100384 | tf_op jit(solution)/shard_map/ppermute | solution.py:110
  15.5 0.1 slice_bitcast_fusion.2
  15.8 1.3 %rev.7 = bf16[48,35,35]{2,1,0:T(8,128)(2,1)S(1)} reverse(bf16[48,35,35]{2,1,0:T(8,128)(2,1)S(1)} %pad_maximum_fusion), dimensions={1} | reverse | bytes 235200 | tf_op jit(solution)/shard_map/rev | solution.py:140
  17.1 1.6 %rev.6 = bf16[48,35,35]{2,1,0:T(8,128)(2,1)S(1)} reverse(bf16[48,35,35]{2,1,0:T(8,128)(2,1)S(1)} %pad_maximum_fusion), dimensions={2} | reverse | bytes 235200 | tf_op jit(solution)/shard_map/rev | solution.py:136
  18.8 1.9 %collective-permute-start.1 = (bf16[32,512]{1,0:T(8,128)(2,1)S(1)}, bf16[32,512]{1,0:T(8,128)(2,1)S(1)}, u32[]{:S(2)}, u32[]{:S(2)}) collective-permute-start(bf16[32,512]{1,0:T(8,128)(2,1)S(1)} %maximum_select_fusion.1.own), channel_id=1, source_target_pairs={{0,32},{32,64},{64,96},{96,128},{128,160},{160,192},{192,224},{1,3... | collective-permute-start | bytes 98312 | tf_op jit(solution)/shard_map/ppermute | solution.py:126
  20.7 3.6 %collective-permute-start.2 = (bf16[32,512]{1,0:T(8,128)(2,1)S(1)}, bf16[32,512]{1,0:T(8,128)(2,1)S(1)}, u32[]{:S(2)}, u32[]{:S(2)}) collective-permute-start(bf16[32,512]{1,0:T(8,128)(2,1)S(1)} %maximum_select_fusion.1.own), channel_id=1, source_target_pairs={{32,0},{64,32},{96,64},{128,96},{160,128},{192,160},{224,192},{33,... | collective-permute-start | bytes 98312 | tf_op jit(solution)/shard_map/ppermute | solution.py:127
  24.4 0.5 copy.15
  24.9 0.3 reshape.34
  25.3 0.1 pad_dynamic-update-slice_fusion.6
  25.5 0.1 pad_dynamic-update-slice_fusion.4
  25.6 0.1 pad_dynamic-update-slice_fusion.3
  26.2 0.3 reshape.33
  27.5 9.6 %shard_map.68 = (f32[32,256]{1,0:T(8,128)S(1)}, f32[32,256]{1,0:T(8,128)S(1)}, f32[32,256]{1,0:T(8,128)S(1)}, f32[32,256]{1,0:T(8,128)S(1)}) custom-call(bf16[32,512]{1,0:T(8,128)(2,1)S(1)} %collective-permute-done.1.top, bf16[32,512]{1,0:T(8,128)(2,1)S(1)} %maximum_select_fusion.1.own, bf16[32,512]{1,0:T(8,128)(2,1)S(1)} %collective-permute-done.2.bot, ...), custom_call_target="tpu_custom_call" | custom-call | tf_op jit(solution)/shard_map/pallas_call | solution.py:152
  37.1 2.2 %collective-permute-start.3 = (f32[32,256]{1,0:T(8,128)S(1)}, f32[32,256]{1,0:T(8,128)S(1)}, u32[]{:S(2)}, u32[]{:S(2)}) collective-permute-start(f32[32,256]{1,0:T(8,128)S(1)} %get-tuple-element.8), channel_id=1, source_target_pairs={{32,0},{64,32},{96,64},{128,96},{160,128},{192,160},{224,192},{33,... | collective-permute-start | bytes 98312 | tf_op jit(solution)/shard_map/ppermute | solution.py:164
  39.3 2.1 %collective-permute-start.4 = (f32[32,256]{1,0:T(8,128)S(1)}, f32[32,256]{1,0:T(8,128)S(1)}, u32[]{:S(2)}, u32[]{:S(2)}) collective-permute-start(f32[32,256]{1,0:T(8,128)S(1)} %get-tuple-element.9), channel_id=1, source_target_pairs={{0,32},{32,64},{64,96},{96,128},{128,160},{160,192},{192,224},{1,3... | collective-permute-start | bytes 98312 | tf_op jit(solution)/shard_map/ppermute | solution.py:165
  41.4 3.1 %collective-permute-done.4 = f32[32,256]{1,0:T(8,128)S(1)} collective-permute-done((f32[32,256]{1,0:T(8,128)S(1)}, f32[32,256]{1,0:T(8,128)S(1)}, u32[]{:S(2)}, u32[]{:S(2)}) %collective-permute-start.4) | collective-permute-done | bytes 32800 | tf_op jit(solution)/shard_map/ppermute | solution.py:165
  44.7 5.8 %collective-permute-done.5 = f32[64,256]{1,0:T(8,128)S(1)} collective-permute-done((f32[64,256]{1,0:T(8,128)S(1)}, f32[64,256]{1,0:T(8,128)S(1)}, u32[]{:S(2)}, u32[]{:S(2)}) %collective-permute-start.5) | collective-permute-done | bytes 65568 | tf_op jit(solution)/shard_map/ppermute | solution.py:169
  50.4 0.7 %fusion.22 = (f32[32,512]{1,0:T(8,128)}, f32[32,512]{1,0:T(8,128)}) fusion(f32[64,512]{1,0:T(8,128)S(1)} %maximum_select_fusion), kind=kLoop, calls=%fused_computation.68 | loop fusion | bytes 262144 | tf_op jit(solution)/shard_map/slice | solution.py:173
  (40 shorter events, 1.9 us)
Async XLA Ops:
  4.3 11.2 %collective-permute-start = (bf16[392,128]{1,0:T(8,128)(2,1)S(1)}, bf16[392,128]{1,0:T(8,128)(2,1)S(1)}, u32[]{:S(2)}, u32[]{:S(2)}) collective-permute-start(bf16[392,128]{1,0:T(8,128)(2,1)S(1)} %pad_maximum_fusion.2), channel_id=1, source_target_pairs={{1,2},{2,1},{3,4},{4,3},{5,6},{6,5},{7,8},{8,7},{9,10},{10,9},{11,... | collective-permute-start | bytes 301064 | tf_op jit(solution)/shard_map/ppermute | solution.py:110
  18.8 8.6 %collective-permute-start.1 = (bf16[32,512]{1,0:T(8,128)(2,1)S(1)}, bf16[32,512]{1,0:T(8,128)(2,1)S(1)}, u32[]{:S(2)}, u32[]{:S(2)}) collective-permute-start(bf16[32,512]{1,0:T(8,128)(2,1)S(1)} %maximum_select_fusion.1.own), channel_id=1, source_target_pairs={{0,32},{32,64},{64,96},{96,128},{128,160},{160,192},{192,224},{1,3... | collective-permute-start | bytes 98312 | tf_op jit(solution)/shard_map/ppermute | solution.py:126
  20.7 6.7 %collective-permute-start.2 = (bf16[32,512]{1,0:T(8,128)(2,1)S(1)}, bf16[32,512]{1,0:T(8,128)(2,1)S(1)}, u32[]{:S(2)}, u32[]{:S(2)}) collective-permute-start(bf16[32,512]{1,0:T(8,128)(2,1)S(1)} %maximum_select_fusion.1.own), channel_id=1, source_target_pairs={{32,0},{64,32},{96,64},{128,96},{160,128},{192,160},{224,192},{33,... | collective-permute-start | bytes 98312 | tf_op jit(solution)/shard_map/ppermute | solution.py:127
  26.1 1.2 %copy-start = (f32[12]{0:T(128)S(1)}, f32[12]{0:T(128)}, u32[]{:S(2)}) copy-start(f32[12]{0:T(128)} %param.9) | copy-start | bytes 148
  37.1 4.4 %collective-permute-start.3 = (f32[32,256]{1,0:T(8,128)S(1)}, f32[32,256]{1,0:T(8,128)S(1)}, u32[]{:S(2)}, u32[]{:S(2)}) collective-permute-start(f32[32,256]{1,0:T(8,128)S(1)} %get-tuple-element.8), channel_id=1, source_target_pairs={{32,0},{64,32},{96,64},{128,96},{160,128},{192,160},{224,192},{33,... | collective-permute-start | bytes 98312 | tf_op jit(solution)/shard_map/ppermute | solution.py:164
  39.3 5.2 %collective-permute-start.4 = (f32[32,256]{1,0:T(8,128)S(1)}, f32[32,256]{1,0:T(8,128)S(1)}, u32[]{:S(2)}, u32[]{:S(2)}) collective-permute-start(f32[32,256]{1,0:T(8,128)S(1)} %get-tuple-element.9), channel_id=1, source_target_pairs={{0,32},{32,64},{64,96},{96,128},{128,160},{160,192},{192,224},{1,3... | collective-permute-start | bytes 98312 | tf_op jit(solution)/shard_map/ppermute | solution.py:165
  44.5 5.9 %collective-permute-start.5 = (f32[64,256]{1,0:T(8,128)S(1)}, f32[64,256]{1,0:T(8,128)S(1)}, u32[]{:S(2)}, u32[]{:S(2)}) collective-permute-start(f32[64,256]{1,0:T(8,128)S(1)} %pad_maximum_fusion.3), channel_id=1, source_target_pairs={{0,1},{1,0},{2,3},{3,2},{4,5},{5,4},{6,7},{7,6},{8,9},{9,8},{10,11... | collective-permute-start | bytes 196616 | tf_op jit(solution)/shard_map/ppermute | solution.py:169

commit v2 on v1

v2 whole, which is shorter than its diff:
```python
import jax
import jax.numpy as jnp
from jax import lax
from jax.experimental import pallas as pl
from jax.experimental.pallas import tpu as pltpu
from jax.sharding import PartitionSpec as P

STEEP = 4.0
THRESHOLD = 1.0
GAIN = 128.0
TAPS = 35
MARGIN = 17
SLOT = 40
BLOCK = 8
ROWS = 32
CHANNELS = 48
FWD_K = 1792
ADJ_K = 2304
LEAD = 6
WIDE = 384
BF = jnp.bfloat16
F32 = jnp.float32
VMEM = pl.BlockSpec(memory_space=pltpu.VMEM)
HBM = pl.BlockSpec(memory_space=pltpu.HBM)


def start_body(levels, offset, bits, strip, full, short, goal, levels_v, offset_v, bits_v, sems):
    moves = [
        pltpu.make_async_copy(a, b, sems.at[n])
        for n, (a, b) in enumerate([(levels, levels_v), (offset, offset_v), (bits, bits_v)])
    ]
    for move in moves:
        move.start()
    left = lax.axis_index("kern") == 0
    for move in moves:
        move.wait()
    value = jax.nn.sigmoid(2.0 * (levels_v[...].astype(F32) - 1.5) + offset_v[...])
    full[...] = value
    want = bits_v[...].astype(F32)
    short[...] = value.astype(BF)
    goal[...] = want.astype(BF)
    low = lax.broadcasted_iota(jnp.int32, (ROWS, 128), 1) < 64
    ends = jnp.where(low, pltpu.roll(value[:, -128:], 64, 1), want[:, -128:])
    starts = jnp.where(low, value[:, :128], pltpu.roll(want[:, :128], 64, 1))
    strip[...] = jnp.where(left, ends, starts).astype(BF)


def pack_body(kernels, weights, after, packed, padded):
    del after
    padded[...] = jnp.zeros((24, 40, 128), F32)
    row = lax.broadcasted_iota(jnp.int32, (8, 128), 0)
    lane = lax.broadcasted_iota(jnp.int32, (8, 128), 1)
    index = lax.rem(3 * row + jnp.maximum(lane - 120, 0), 12)
    table = jnp.zeros((8, 128), F32)
    for n in range(12):
        table = jnp.where(index == n, weights[n], table)
    table = jnp.where((lane >= 120) & (lane < 123), table, 0.0)
    high = table.astype(BF).astype(F32)
    middle = (table - high).astype(BF).astype(F32)
    lower = table - high - middle
    for n in range(24):
        padded[n, 0:TAPS, 0:TAPS] = kernels[n].astype(F32)
    for g in range(8):
        tile = padded[3 * g]
        tile = tile + pltpu.roll(padded[3 * g + 1], 40, 1)
        tile = tile + pltpu.roll(padded[3 * g + 2], 80, 1)
        extra = jnp.where(
            row == 0, high[g : g + 1], jnp.where(row == 1, middle[g : g + 1], lower[g : g + 1])
        )
        extra = jnp.where(row < 3, extra, 0.0)
        tile = jnp.concatenate([tile[:8] + extra, tile[8:]], axis=0)
        packed[40 * g : 40 * g + 40, :] = tile.astype(BF)


def shifted(tiles, shift, count, lane):
    skip, rest = divmod(shift, 128)
    if rest:
        turned = [None if t is None else pltpu.roll(t, rest, 1) for t in tiles]
    else:
        turned = tiles
    get = lambda n: turned[n] if 0 <= n < len(turned) else None
    out = []
    for n in range(count):
        here = get(n - skip)
        if rest:
            before = get(n - skip - 1)
            if here is not None and before is not None:
                here = jnp.where(lane >= rest, here, before)
            elif here is not None:
                here = jnp.where(lane >= rest, here, 0.0)
            elif before is not None:
                here = jnp.where(lane < rest, before, 0.0)
        out.append(here)
    return out


def taps_body(mine, theirs, fwd, adj, wgt, plain, flipped):
    row = lax.broadcasted_iota(jnp.int32, (128, 128), 0)
    column = lax.broadcasted_iota(jnp.int32, (128, 128), 1)
    group = jnp.where(row >= 80, 2, jnp.where(row >= 40, 1, 0))
    flip = (row + column == 80 * group + 34) & (row < 40 * group + TAPS)
    flip = flip.astype(F32).astype(BF)
    for p, source in enumerate((mine, theirs)):
        block = source[...]
        plain[320 * p : 320 * p + 320, :] = block.astype(F32)
        flipped[320 * p : 320 * p + 320, :] = jnp.dot(block, flip, preferred_element_type=F32)

    def pick(ref, a):
        return jnp.concatenate(
            [ref[pl.ds(a, 8, stride=40), :], ref[pl.ds(320 + a, 8, stride=40), :]], axis=0
        )

    parts = (pick(plain, 0) + pick(plain, 1)) + pick(plain, 2)
    for i in range(3):
        wgt[16 * i : 16 * i + 16, :] = jnp.broadcast_to(parts[:, 120 + i : 121 + i], (16, WIDE))
    lane = lax.broadcasted_iota(jnp.int32, (16, 128), 1)
    empty = jnp.zeros((16, 128), BF)
    for i in range(3):
        tiles = [None] * 11
        for a in range(TAPS):
            first, off = divmod(SLOT * a, 128)
            turned = pick(flipped, a)
            if (off - SLOT * i) % 128:
                turned = pltpu.roll(turned, (off - SLOT * i) % 128, 1)
            inside = min(SLOT, 128 - off)
            piece = jnp.where((lane >= off) & (lane < off + inside), turned, 0.0)
            tiles[first] = piece if tiles[first] is None else tiles[first] + piece
            if inside < SLOT:
                piece = jnp.where(lane < SLOT - inside, turned, 0.0)
                tiles[first + 1] = piece
        for x in range(BLOCK):
            top = 128 * i + 16 * x
            for n, tile in enumerate(shifted(tiles, SLOT * x, 14, lane)):
                fwd[top : top + 16, 128 * n : 128 * n + 128] = (
                    empty if tile is None else tile.astype(BF)
                )
    turned = []
    for q in range(5):
        lines = []
        for e in range(8):
            a = TAPS - 1 - 8 * q - e
            lines.append(pick(plain, a) if a >= 0 else jnp.zeros((16, 128), F32))
        turned.append(jnp.transpose(jnp.concatenate(lines, axis=0)))
    lane = lax.broadcasted_iota(jnp.int32, (SLOT, 128), 1)
    zero = jnp.zeros((SLOT, 128), F32)
    for i in range(3):
        tiles = [t[SLOT * i : SLOT * i + SLOT] for t in turned]
        for x in range(0, BLOCK, 2):
            a = shifted(tiles, 16 * (x + LEAD), 6, lane)
            b = shifted(tiles, 16 * (x + 1 + LEAD), 6, lane)
            for n in range(6):
                both = [zero if t is None else t for t in (a[n], b[n])]
                at = 128 * (3 * n + i)
                adj[SLOT * x : SLOT * (x + 2), at : at + 128] = jnp.concatenate(both, axis=0).astype(BF)


def share(adj, charge, j):
    low = max(0, 40 - 8 * j)
    high = min(48, 72 - 8 * j)
    first = low - 40 + 8 * j
    return jnp.dot(
        adj[:, 48 * low : 48 * high],
        charge[48 * first : 48 * (first + high - low), :],
        preferred_element_type=F32,
    )


def fold(part, i):
    moved = pltpu.roll(part[SLOT * i : SLOT * i + SLOT], 0, 1, stride=1, stride_axis=0)
    line = jnp.sum(moved, axis=0, keepdims=True)
    return pltpu.roll(line, WIDE - 34, 1)[:, :256]


def main_body(one, own, two, tgt, wgt, fwd, adj, res_out, one_out, two_out, some_out, charge, rows, image, up_out, dn_out):
    even = lax.rem(lax.axis_index("row"), 2) == 0
    below = one[...].astype(F32)
    above = two[...].astype(F32)
    rows[0:32, :] = jnp.where(even, above, below)
    rows[32:64, :] = own[...].astype(F32)
    rows[64:96, :] = jnp.where(even, below, above)
    image[2640:2752, :] = jnp.zeros((112, WIDE), BF)
    for p in range(33):
        parts = []
        for i in range(2):
            line = jnp.broadcast_to(rows[15 + 2 * p + i : 16 + 2 * p + i, :], (SLOT, 512))
            parts.append(pltpu.roll(line, 0, 1, stride=1, stride_axis=0)[:, 128:])
        image[80 * p : 80 * p + 80, :] = jnp.concatenate(parts, axis=0).astype(BF)
    weight = wgt[...].reshape(3, 1, 16, WIDE)
    goal = pltpu.roll(tgt[...].astype(F32), 512 - 111, 1)[:, :WIDE]
    for j in range(4):
        fields = jnp.dot(fwd[...], image[320 * j : 320 * j + FWD_K, :], preferred_element_type=F32)
        fields = fields.reshape(3, BLOCK, 16, WIDE)
        squares = weight * fields * fields
        intensity = jnp.sum((squares[0] + squares[1]) + squares[2], axis=1)
        resist = jax.nn.sigmoid(STEEP * (intensity - THRESHOLD))
        want = goal[8 * j : 8 * j + 8]
        slope = GAIN * (resist - want) * resist * (1.0 - resist)
        slope = jnp.where(want > 1.5, 0.0, slope)
        scaled = (2.0 * weight) * slope[None, :, None, :] * fields
        charge[384 * j : 384 * j + 384, :] = scaled.reshape(384, WIDE).astype(BF)
        res_out[8 * j : 8 * j + 8, :] = pltpu.roll(resist, WIDE - MARGIN, 1)[:, :256]
    up_out[0:15, :] = jnp.zeros((15, 256), F32)
    dn_out[17:32, :] = jnp.zeros((15, 256), F32)
    for j in (0, 1, 2, 6, 7, 8):
        part = share(adj, charge, j)
        for i in range(BLOCK):
            x = 8 * j + i - MARGIN
            if x < 0:
                up_out[ROWS + x : ROWS + x + 1, :] = fold(part, i)
            elif ROWS <= x <= ROWS + MARGIN - 1:
                dn_out[x - ROWS : x - ROWS + 1, :] = fold(part, i)
            elif 0 <= x < ROWS:
                some_out[x : x + 1, :] = fold(part, i)
    one_out[...] = jnp.where(even, dn_out[...], up_out[...])
    two_out[...] = jnp.where(even, up_out[...], dn_out[...])


def rest_body(adj, charge, some, mid_out):
    mid_out[0:7, :] = some[0:7, :]
    mid_out[31:32, :] = some[31:32, :]
    for j in (3, 4, 5):
        part = share(adj, charge, j)
        for i in range(BLOCK):
            x = 8 * j + i - MARGIN
            if 0 <= x < ROWS:
                mid_out[x : x + 1, :] = fold(part, i)


def per_device(mask_levels, level_offset, target_bits, socs_kernels, kernel_weights):
    kern = lax.axis_index("kern")
    col = lax.axis_index("col")
    n_row, n_col = lax.axis_size("row"), lax.axis_size("col")
    left = kern == 0
    wide = lambda dtype: jax.ShapeDtypeStruct((ROWS, 512), dtype)
    strip, mask_full, mask_bf, target = pl.pallas_call(
        start_body,
        out_shape=(jax.ShapeDtypeStruct((ROWS, 128), BF), wide(F32), wide(BF), wide(BF)),
        in_specs=[HBM] * 3,
        out_specs=(VMEM,) * 4,
        scratch_shapes=[
            pltpu.VMEM((ROWS, 512), jnp.int32),
            pltpu.VMEM((ROWS, 512), F32),
            pltpu.VMEM((ROWS, 512), jnp.int32),
            pltpu.SemaphoreType.DMA((3,)),
        ],
        compiler_params=pltpu.CompilerParams(vmem_limit_bytes=16 * 2**20),
        name="start",
    )(mask_levels, level_offset, target_bits)
    to_right = [(2 * c, 2 * c + 2) for c in range(n_col - 1)]
    to_left = [(2 * c + 3, 2 * c + 1) for c in range(n_col - 1)]
    strip_in = lax.ppermute(strip, ("col", "kern"), to_right + to_left)
    kernels, _ = lax.optimization_barrier((socs_kernels, strip))
    packed = pl.pallas_call(
        pack_body,
        out_shape=jax.ShapeDtypeStruct((320, 128), BF),
        in_specs=[VMEM, pl.BlockSpec(memory_space=pltpu.SMEM), VMEM],
        out_specs=VMEM,
        scratch_shapes=[pltpu.VMEM((24, 40, 128), F32)],
        compiler_params=pltpu.CompilerParams(vmem_limit_bytes=16 * 2**20),
        cost_estimate=pl.CostEstimate(flops=10**6, bytes_accessed=3 * 10**5, transcendentals=0),
        name="pack",
    )(kernels.reshape(24, TAPS, TAPS), kernel_weights, strip)
    swap = [(0, 1), (1, 0)]
    other = lax.ppermute(packed, "kern", swap)
    outside = jnp.where(left, col == 0, col == n_col - 1)
    edge_mask = jnp.where(outside, jnp.zeros((), BF), strip_in[:, :64])
    edge_target = jnp.where(outside, jnp.full((), 2.0, BF), strip_in[:, 64:])
    blank = jnp.zeros((ROWS, 64), BF)

    def window(value, edge):
        return jnp.where(
            left,
            jnp.concatenate([blank, edge, value[:, :384]], axis=1),
            jnp.concatenate([value[:, 128:], edge, blank], axis=1),
        )

    own = window(mask_bf, edge_mask)
    goal = window(target, edge_target)
    near = [(i, i ^ 1) for i in range(n_row)]
    far = [(i, ((i + 1) ^ 1) - 1) for i in range(1, n_row - 1)]
    one = lax.ppermute(own, "row", near)
    two = lax.ppermute(own, "row", far)
    fwd, adj, weights = pl.pallas_call(
        taps_body,
        out_shape=(
            jax.ShapeDtypeStruct((384, FWD_K), BF),
            jax.ShapeDtypeStruct((SLOT * BLOCK, ADJ_K), BF),
            jax.ShapeDtypeStruct((CHANNELS, WIDE), F32),
        ),
        in_specs=[VMEM] * 2,
        out_specs=(VMEM,) * 3,
        scratch_shapes=[pltpu.VMEM((640, 128), F32), pltpu.VMEM((640, 128), F32)],
        compiler_params=pltpu.CompilerParams(vmem_limit_bytes=16 * 2**20),
        cost_estimate=pl.CostEstimate(flops=4 * 10**8, bytes_accessed=4 * 10**6, transcendentals=0),
        name="taps",
    )(packed, other)
    tile = jax.ShapeDtypeStruct((ROWS, 256), F32)
    resist, share_one, share_two, some, charge = pl.pallas_call(
        main_body,
        out_shape=(tile, tile, tile, tile, jax.ShapeDtypeStruct((1536, WIDE), BF)),
        in_specs=[VMEM] * 7,
        out_specs=(VMEM,) * 5,
        scratch_shapes=[
            pltpu.VMEM((96, 512), F32),
            pltpu.VMEM((2752, WIDE), BF),
            pltpu.VMEM((ROWS, 256), F32),
            pltpu.VMEM((ROWS, 256), F32),
        ],
        compiler_params=pltpu.CompilerParams(vmem_limit_bytes=24 * 2**20),
        cost_estimate=pl.CostEstimate(flops=6 * 10**9, bytes_accessed=6 * 10**6, transcendentals=0),
        name="fields",
    )(one, own, two, goal, weights, fwd, adj)
    got_one = lax.ppermute(share_one, "row", near)
    got_two = lax.ppermute(share_two, "row", far)
    middle_rows = pl.pallas_call(
        rest_body,
        out_shape=tile,
        in_specs=[VMEM] * 3,
        out_specs=VMEM,
        compiler_params=pltpu.CompilerParams(vmem_limit_bytes=16 * 2**20),
        cost_estimate=pl.CostEstimate(flops=2 * 10**9, bytes_accessed=3 * 10**6, transcendentals=0),
        name="inner",
    )(adj, charge, some)
    half = jnp.where(left, mask_full[:, :256], mask_full[:, 256:])
    gradient = (middle_rows + got_one + got_two) * half * (1.0 - half)
    mine = jnp.concatenate([resist, gradient], axis=0)
    theirs = lax.ppermute(mine, "kern", swap)
    both = jnp.where(
        left, jnp.concatenate([mine, theirs], axis=1), jnp.concatenate([theirs, mine], axis=1)
    )
    return both[:ROWS], both[ROWS:]


def solution(mesh):
    return jax.shard_map(
        per_device,
        mesh=mesh,
        in_specs=(
            P("row", "col"),
            P("row", "col"),
            P("row", "col"),
            P(None, "kern", None, None),
            P("kern"),
        ),
        out_specs=(P("row", "col"), P("row", "col")),
        check_vma=False,
    )
```

time: 51.4 us -> 39.2 us (0.76)
  the two profiles are of different devices: /device:TPU:6 before, /device:TPU:10 now
where the time goes in v2:
time: 39.2 us; the launch traced here: 38.9 us
  starting transfers between devices  17.9 us (46%)
  Pallas kernels  9.28 us (24%)
  waiting for transfers between devices  5.97 us (15%)
  local copies, waits for them, and re-layouts  4.81 us (12%)
  between operations  0.75 us (2%)
    ppermute x1, starting transfers between devices, per_device(): other = lax.ppermute(packed, 'kern', swap)  6.5 us
    pallas_call x1, Pallas kernels, per_device(): pl.pallas_call(main_body, out_shape=(tile, tile, tile, tile, jax.ShapeDty...  5.1 us
    ppermute x1, waiting for transfers between devices, per_device(): theirs = lax.ppermute(mine, 'kern', swap)  4.3 us
    ppermute x1, starting transfers between devices, per_device(): strip_in = lax.ppermute(strip, ('col', 'kern'), to_right + to_left)  3.83 us
    unnamed x8, local copies, waits for them, and re-layouts  3.16 us
    ppermute x1, starting transfers between devices, per_device(): got_two = lax.ppermute(share_two, 'row', far)  2.05 us
    ppermute x1, starting transfers between devices, per_device(): two = lax.ppermute(own, 'row', far)  1.92 us
    pallas_call x1, Pallas kernels, per_device(): pl.pallas_call(rest_body, out_shape=tile, in_specs=[VMEM] * 3, out_specs=...  1.91 us
  transfers between devices with their start and end apart: 7, of which 3 were waited for; matrix products, arithmetic and copies ran while one was open for 3% of the time, Pallas kernels for 10%

profile of v2, /device:TPU:10, one launch (start us, length us, event | category | flops | bytes accessed | tf_op | source)
XLA Modules:
  0.0 38.9 jit_solution(1232435977992172843)
XLA Ops:
  0.6 0.8 %copy-done = s32[32,512]{1,0:T(8,128)S(1)} copy-done((s32[32,512]{1,0:T(8,128)S(1)}, s32[32,512]{1,0:T(8,128)}, u32[]{:S(2)}) %copy-start) | copy-done | bytes 65560
  1.5 0.8 %copy-done.1 = f32[32,512]{1,0:T(8,128)S(1)} copy-done((f32[32,512]{1,0:T(8,128)S(1)}, f32[32,512]{1,0:T(8,128)}, u32[]{:S(2)}) %copy-start.1) | copy-done | bytes 65560
  2.3 0.8 %copy-done.2 = s32[32,512]{1,0:T(8,128)S(1)} copy-done((s32[32,512]{1,0:T(8,128)S(1)}, s32[32,512]{1,0:T(8,128)}, u32[]{:S(2)}) %copy-start.2) | copy-done | bytes 65560
  3.2 0.3 start.1
  3.5 3.8 %collective-permute-start = (bf16[32,128]{1,0:T(8,128)(2,1)S(1)}, bf16[32,128]{1,0:T(8,128)(2,1)S(1)}, u32[]{:S(2)}, u32[]{:S(2)}) collective-permute-start(bf16[32,128]{1,0:T(8,128)(2,1)S(1)} %get-tuple-element.15.after), channel_id=1, source_target_pairs={{0,2},{2,4},{4,6},{6,8},{8,10},{10,12},{12,14},{14,16},{16,18},{18... | collective-permute-start | bytes 24584 | tf_op jit(solution)/shard_map/ppermute | solution.py:251
  7.3 1.0 %copy.7 = bf16[2,12,35,35]{3,2,1,0:T(8,128)(2,1)S(1)} copy(bf16[2,12,35,35]{3,0,2,1:T(2,128)(2,1)} %param.8) | data formatting | bytes 117600 | tf_op jit(solution)/shard_map/optimization_barrier | solution.py:252
  8.3 0.0 copy-start.3
  8.3 0.6 %copy-done.3 = f32[12]{0:T(128)S(1)} copy-done((f32[12]{0:T(128)S(1)}, f32[12]{0:T(128)}, u32[]{:S(2)}) %copy-start.3) | copy-done | bytes 72
  9.0 0.7 %pack.1.mine = bf16[320,128]{1,0:T(8,128)(2,1)S(1)} custom-call(bf16[24,35,35]{2,1,0:T(8,128)(2,1)S(1)} %bitcast.1, f32[12]{0:T(128)S(1)} %copy-done.3, bf16[32,128]{1,0:T(8,128)(2,1)S(1)} %get-tuple-element.15.after), custom_call_target="tpu_custom_call" | custom-call | flops 1000000 | bytes 300000 | tf_op jit(solution)/shard_map/pack/pallas_call | solution.py:253
  9.7 6.5 %collective-permute-start.3 = (bf16[320,128]{1,0:T(8,128)(2,1)S(1)}, bf16[320,128]{1,0:T(8,128)(2,1)S(1)}, u32[]{:S(2)}, u32[]{:S(2)}) collective-permute-start(bf16[320,128]{1,0:T(8,128)(2,1)S(1)} %pack.1.mine), channel_id=1, source_target_pairs={{0,1},{1,0},{2,3},{3,2},{4,5},{5,4},{6,7},{7,6},{8,9},{9,8},{10,11... | collective-permute-start | bytes 245768 | tf_op jit(solution)/shard_map/ppermute | solution.py:264
  16.2 0.1 slice_select_fusion
  16.3 0.1 fusion.1
  16.4 1.9 %collective-permute-start.2 = (bf16[32,512]{1,0:T(8,128)(2,1)S(1)}, bf16[32,512]{1,0:T(8,128)(2,1)S(1)}, u32[]{:S(2)}, u32[]{:S(2)}) collective-permute-start(bf16[32,512]{1,0:T(8,128)(2,1)S(1)} %get-tuple-element.35.own), channel_id=1, source_target_pairs={{32,64},{64,32},{96,128},{128,96},{160,192},{192,160},{33,65},{65,... | collective-permute-start | bytes 98312 | tf_op jit(solution)/shard_map/ppermute | solution.py:282
  18.4 1.7 %collective-permute-start.1 = (bf16[32,512]{1,0:T(8,128)(2,1)S(1)}, bf16[32,512]{1,0:T(8,128)(2,1)S(1)}, u32[]{:S(2)}, u32[]{:S(2)}) collective-permute-start(bf16[32,512]{1,0:T(8,128)(2,1)S(1)} %get-tuple-element.35.own), channel_id=1, source_target_pairs={{0,32},{32,0},{64,96},{96,64},{128,160},{160,128},{192,224},{224,1... | collective-permute-start | bytes 98312 | tf_op jit(solution)/shard_map/ppermute | solution.py:281
  20.0 1.2 %taps.1 = (bf16[384,1792]{1,0:T(8,128)(2,1)S(1)}, bf16[320,2304]{1,0:T(8,128)(2,1)S(1)}, f32[48,384]{1,0:T(8,128)S(1)}) custom-call(bf16[320,128]{1,0:T(8,128)(2,1)S(1)} %pack.1.mine, bf16[320,128]{1,0:T(8,128)(2,1)S(1)} %collective-permute-done.3.theirs), custom_call_target="tpu_custom_call" | custom-call | flops 400000000 | bytes 4000000 | tf_op jit(solution)/shard_map/taps/pallas_call | solution.py:283
  21.2 0.4 %collective-permute-done.2.two = bf16[32,512]{1,0:T(8,128)(2,1)S(1)} collective-permute-done((bf16[32,512]{1,0:T(8,128)(2,1)S(1)}, bf16[32,512]{1,0:T(8,128)(2,1)S(1)}, u32[]{:S(2)}, u32[]{:S(2)}) %collective-permute-start.2) | collective-permute-done | bytes 32800 | tf_op jit(solution)/shard_map/ppermute | solution.py:282
  21.7 5.1 %fields.1 = (f32[32,256]{1,0:T(8,128)S(1)}, f32[32,256]{1,0:T(8,128)S(1)}, f32[32,256]{1,0:T(8,128)S(1)}, f32[32,256]{1,0:T(8,128)S(1)}, bf16[1536,384]{1,0:T(8,128)(2,1)S(1)}) custom-call(bf16[32,512]{1,0:T(8,128)(2,1)S(1)} %collective-permute-done.1.one, bf16[32,512]{1,0:T(8,128)(2,1)S(1)} %get-tuple-element.35.own, ...), custom_call_target="tpu_custom_call" | custom-call | flops 6000000000 | bytes 6000000 | tf_op jit(solution)/shard_map/fields/pallas_call | solution.py:298
  26.8 0.2 collective-permute-start.4
  27.0 2.0 %collective-permute-start.5 = (f32[32,256]{1,0:T(8,128)S(1)}, f32[32,256]{1,0:T(8,128)S(1)}, u32[]{:S(2)}, u32[]{:S(2)}) collective-permute-start(f32[32,256]{1,0:T(8,128)S(1)} %get-tuple-element.26), channel_id=1, source_target_pairs={{32,64},{64,32},{96,128},{128,96},{160,192},{192,160},{33,65},{65,... | collective-permute-start | bytes 98312 | tf_op jit(solution)/shard_map/ppermute | solution.py:314
  29.0 1.9 %inner.1 = f32[32,256]{1,0:T(8,128)S(1)} custom-call(bf16[320,2304]{1,0:T(8,128)(2,1)S(1)} %get-tuple-element.21.adj, bf16[1536,384]{1,0:T(8,128)(2,1)S(1)} %get-tuple-element.23.charge, f32[32,256]{1,0:T(8,128)S(1)} %get-tuple-element.24.some), custom_call_target="tpu_custom_call" | custom-call | flops 2000000000 | bytes 3000000 | tf_op jit(solution)/shard_map/inner/pallas_call | solution.py:315
  30.9 1.3 %collective-permute-done.5 = f32[32,256]{1,0:T(8,128)S(1)} collective-permute-done((f32[32,256]{1,0:T(8,128)S(1)}, f32[32,256]{1,0:T(8,128)S(1)}, u32[]{:S(2)}, u32[]{:S(2)}) %collective-permute-start.5) | collective-permute-done | bytes 32800 | tf_op jit(solution)/shard_map/ppermute | solution.py:314
  32.2 1.7 %collective-permute-start.6 = (f32[64,256]{1,0:T(8,128)S(1)}, f32[64,256]{1,0:T(8,128)S(1)}, u32[]{:S(2)}, u32[]{:S(2)}) collective-permute-start(f32[64,256]{1,0:T(8,128)S(1)} %pad_maximum_fusion), channel_id=1, source_target_pairs={{0,1},{1,0},{2,3},{3,2},{4,5},{5,4},{6,7},{7,6},{8,9},{9,8},{10,11... | collective-permute-start | bytes 196616 | tf_op jit(solution)/shard_map/ppermute | solution.py:327
  33.9 4.3 %collective-permute-done.6 = f32[64,256]{1,0:T(8,128)S(1)} collective-permute-done((f32[64,256]{1,0:T(8,128)S(1)}, f32[64,256]{1,0:T(8,128)S(1)}, u32[]{:S(2)}, u32[]{:S(2)}) %collective-permute-start.6) | collective-permute-done | bytes 65568 | tf_op jit(solution)/shard_map/ppermute | solution.py:327
  38.3 0.7 %fusion.4 = (f32[32,512]{1,0:T(8,128)}, f32[32,512]{1,0:T(8,128)}) fusion(f32[64,512]{1,0:T(8,128)S(1)} %maximum_select_fusion), kind=kLoop, calls=%fused_computation.13 | loop fusion | bytes 262144 | tf_op jit(solution)/shard_map/slice | solution.py:331
  (12 shorter events, 0.1 us)
Async XLA Ops:
  0.6 0.8 %copy-start = (s32[32,512]{1,0:T(8,128)S(1)}, s32[32,512]{1,0:T(8,128)}, u32[]{:S(2)}) copy-start(s32[32,512]{1,0:T(8,128)} %levels.1) | copy-start | bytes 196612
  1.5 0.8 %copy-start.1 = (f32[32,512]{1,0:T(8,128)S(1)}, f32[32,512]{1,0:T(8,128)}, u32[]{:S(2)}) copy-start(f32[32,512]{1,0:T(8,128)} %offset.1) | copy-start | bytes 196612
  2.3 0.8 %copy-start.2 = (s32[32,512]{1,0:T(8,128)S(1)}, s32[32,512]{1,0:T(8,128)}, u32[]{:S(2)}) copy-start(s32[32,512]{1,0:T(8,128)} %bits.1) | copy-start | bytes 196612
  3.5 12.7 %collective-permute-start = (bf16[32,128]{1,0:T(8,128)(2,1)S(1)}, bf16[32,128]{1,0:T(8,128)(2,1)S(1)}, u32[]{:S(2)}, u32[]{:S(2)}) collective-permute-start(bf16[32,128]{1,0:T(8,128)(2,1)S(1)} %get-tuple-element.15.after), channel_id=1, source_target_pairs={{0,2},{2,4},{4,6},{6,8},{8,10},{10,12},{12,14},{14,16},{16,18},{18... | collective-permute-start | bytes 24584 | tf_op jit(solution)/shard_map/ppermute | solution.py:251
  8.3 0.7 %copy-start.3 = (f32[12]{0:T(128)S(1)}, f32[12]{0:T(128)}, u32[]{:S(2)}) copy-start(f32[12]{0:T(128)} %weights.1) | copy-start | bytes 148
  9.7 10.3 %collective-permute-start.3 = (bf16[320,128]{1,0:T(8,128)(2,1)S(1)}, bf16[320,128]{1,0:T(8,128)(2,1)S(1)}, u32[]{:S(2)}, u32[]{:S(2)}) collective-permute-start(bf16[320,128]{1,0:T(8,128)(2,1)S(1)} %pack.1.mine), channel_id=1, source_target_pairs={{0,1},{1,0},{2,3},{3,2},{4,5},{5,4},{6,7},{7,6},{8,9},{9,8},{10,11... | collective-permute-start | bytes 245768 | tf_op jit(solution)/shard_map/ppermute | solution.py:264
  16.4 5.2 %collective-permute-start.2 = (bf16[32,512]{1,0:T(8,128)(2,1)S(1)}, bf16[32,512]{1,0:T(8,128)(2,1)S(1)}, u32[]{:S(2)}, u32[]{:S(2)}) collective-permute-start(bf16[32,512]{1,0:T(8,128)(2,1)S(1)} %get-tuple-element.35.own), channel_id=1, source_target_pairs={{32,64},{64,32},{96,128},{128,96},{160,192},{192,160},{33,65},{65,... | collective-permute-start | bytes 98312 | tf_op jit(solution)/shard_map/ppermute | solution.py:282
  18.4 3.3 %collective-permute-start.1 = (bf16[32,512]{1,0:T(8,128)(2,1)S(1)}, bf16[32,512]{1,0:T(8,128)(2,1)S(1)}, u32[]{:S(2)}, u32[]{:S(2)}) collective-permute-start(bf16[32,512]{1,0:T(8,128)(2,1)S(1)} %get-tuple-element.35.own), channel_id=1, source_target_pairs={{0,32},{32,0},{64,96},{96,64},{128,160},{160,128},{192,224},{224,1... | collective-permute-start | bytes 98312 | tf_op jit(solution)/shard_map/ppermute | solution.py:281
  26.8 4.2 %collective-permute-start.4 = (f32[32,256]{1,0:T(8,128)S(1)}, f32[32,256]{1,0:T(8,128)S(1)}, u32[]{:S(2)}, u32[]{:S(2)}) collective-permute-start(f32[32,256]{1,0:T(8,128)S(1)} %get-tuple-element.25), channel_id=1, source_target_pairs={{0,32},{32,0},{64,96},{96,64},{128,160},{160,128},{192,224},{224,1... | collective-permute-start | bytes 98312 | tf_op jit(solution)/shard_map/ppermute | solution.py:313
  27.0 5.2 %collective-permute-start.5 = (f32[32,256]{1,0:T(8,128)S(1)}, f32[32,256]{1,0:T(8,128)S(1)}, u32[]{:S(2)}, u32[]{:S(2)}) collective-permute-start(f32[32,256]{1,0:T(8,128)S(1)} %get-tuple-element.26), channel_id=1, source_target_pairs={{32,64},{64,32},{96,128},{128,96},{160,192},{192,160},{33,65},{65,... | collective-permute-start | bytes 98312 | tf_op jit(solution)/shard_map/ppermute | solution.py:314
  32.2 6.0 %collective-permute-start.6 = (f32[64,256]{1,0:T(8,128)S(1)}, f32[64,256]{1,0:T(8,128)S(1)}, u32[]{:S(2)}, u32[]{:S(2)}) collective-permute-start(f32[64,256]{1,0:T(8,128)S(1)} %pad_maximum_fusion), channel_id=1, source_target_pairs={{0,1},{1,0},{2,3},{3,2},{4,5},{5,4},{6,7},{7,6},{8,9},{9,8},{10,11... | collective-permute-start | bytes 196616 | tf_op jit(solution)/shard_map/ppermute | solution.py:327

commit v3 on v2

--- a/solution.py
+++ b/solution.py
@@ -18,21 +18,23 @@
 ADJ_K = 2304
 LEAD = 6
 WIDE = 384
+START_VMEM = 58 * 2**20
 BF = jnp.bfloat16
 F32 = jnp.float32
 VMEM = pl.BlockSpec(memory_space=pltpu.VMEM)
 HBM = pl.BlockSpec(memory_space=pltpu.HBM)
 
 
-def start_body(levels, offset, bits, strip, full, short, goal, levels_v, offset_v, bits_v, sems):
-    moves = [
-        pltpu.make_async_copy(a, b, sems.at[n])
-        for n, (a, b) in enumerate([(levels, levels_v), (offset, offset_v), (bits, bits_v)])
-    ]
+def start_body(levels, offset, bits, kernels, weights, strip, full, short, goal, packed,
+               levels_v, offset_v, bits_v, kernels_v, weights_v, lines, sems):
+    sources = (kernels, weights, levels, offset, bits)
+    targets = (kernels_v, weights_v, levels_v, offset_v, bits_v)
+    moves = [pltpu.make_async_copy(a, b, sems.at[n]) for n, (a, b) in enumerate(zip(sources, targets))]
     for move in moves:
         move.start()
+    lines[...] = jnp.zeros((840, 128), F32)
     left = lax.axis_index("kern") == 0
-    for move in moves:
+    for move in moves[2:]:
         move.wait()
     value = jax.nn.sigmoid(2.0 * (levels_v[...].astype(F32) - 1.5) + offset_v[...])
     full[...] = value
@@ -43,27 +45,27 @@
     ends = jnp.where(low, pltpu.roll(value[:, -128:], 64, 1), want[:, -128:])
     starts = jnp.where(low, value[:, :128], pltpu.roll(want[:, :128], 64, 1))
     strip[...] = jnp.where(left, ends, starts).astype(BF)
-
-
-def pack_body(kernels, weights, after, packed, padded):
-    del after
-    padded[...] = jnp.zeros((24, 40, 128), F32)
+    for move in moves[:2]:
+        move.wait()
+    for n in range(12):
+        lines[70 * n : 70 * n + 70, 0:TAPS] = kernels_v[n].astype(F32).reshape(70, TAPS)
     row = lax.broadcasted_iota(jnp.int32, (8, 128), 0)
     lane = lax.broadcasted_iota(jnp.int32, (8, 128), 1)
-    index = lax.rem(3 * row + jnp.maximum(lane - 120, 0), 12)
+    index = 4 * jnp.maximum(lane - 120, 0) + lax.div(row, 2)
     table = jnp.zeros((8, 128), F32)
     for n in range(12):
-        table = jnp.where(index == n, weights[n], table)
+        table = jnp.where(index == n, weights_v[n], table)
     table = jnp.where((lane >= 120) & (lane < 123), table, 0.0)
     high = table.astype(BF).astype(F32)
     middle = (table - high).astype(BF).astype(F32)
     lower = table - high - middle
-    for n in range(24):
-        padded[n, 0:TAPS, 0:TAPS] = kernels[n].astype(F32)
+    blank = jnp.zeros((SLOT - TAPS, 128), F32)
     for g in range(8):
-        tile = padded[3 * g]
-        tile = tile + pltpu.roll(padded[3 * g + 1], 40, 1)
-        tile = tile + pltpu.roll(padded[3 * g + 2], 80, 1)
+        at = 70 * (g // 2) + g % 2
+        tile = lines[pl.ds(at, TAPS, stride=2), :]
+        tile = tile + pltpu.roll(lines[pl.ds(at + 280, TAPS, stride=2), :], 40, 1)
+        tile = tile + pltpu.roll(lines[pl.ds(at + 560, TAPS, stride=2), :], 80, 1)
+        tile = jnp.concatenate([tile, blank], axis=0)
         extra = jnp.where(
             row == 0, high[g : g + 1], jnp.where(row == 1, middle[g : g + 1], lower[g : g + 1])
         )
@@ -232,34 +234,32 @@
     n_row, n_col = lax.axis_size("row"), lax.axis_size("col")
     left = kern == 0
     wide = lambda dtype: jax.ShapeDtypeStruct((ROWS, 512), dtype)
-    strip, mask_full, mask_bf, target = pl.pallas_call(
+    strip, mask_full, mask_bf, target, packed = pl.pallas_call(
         start_body,
-        out_shape=(jax.ShapeDtypeStruct((ROWS, 128), BF), wide(F32), wide(BF), wide(BF)),
-        in_specs=[HBM] * 3,
-        out_specs=(VMEM,) * 4,
+        out_shape=(
+            pltpu.VMEM((ROWS, 128), BF),
+            pltpu.VMEM((ROWS, 512), F32),
+            pltpu.VMEM((ROWS, 512), BF),
+            pltpu.VMEM((ROWS, 512), BF),
+            pltpu.VMEM((320, 128), BF),
+        ),
+        in_specs=[HBM] * 5,
+        out_specs=(VMEM,) * 5,
         scratch_shapes=[
             pltpu.VMEM((ROWS, 512), jnp.int32),
             pltpu.VMEM((ROWS, 512), F32),
             pltpu.VMEM((ROWS, 512), jnp.int32),
-            pltpu.SemaphoreType.DMA((3,)),
+            pltpu.VMEM((12, TAPS, 2, TAPS), BF),
+            pltpu.SMEM((12,), F32),
+            pltpu.VMEM((840, 128), F32),
+            pltpu.SemaphoreType.DMA((5,)),
         ],
-        compiler_params=pltpu.CompilerParams(vmem_limit_bytes=16 * 2**20),
+        compiler_params=pltpu.CompilerParams(vmem_limit_bytes=START_VMEM),
         name="start",
-    )(mask_levels, level_offset, target_bits)
+    )(mask_levels, level_offset, target_bits, jnp.transpose(socs_kernels, (1, 2, 0, 3)), kernel_weights)
     to_right = [(2 * c, 2 * c + 2) for c in range(n_col - 1)]
     to_left = [(2 * c + 3, 2 * c + 1) for c in range(n_col - 1)]
     strip_in = lax.ppermute(strip, ("col", "kern"), to_right + to_left)
-    kernels, _ = lax.optimization_barrier((socs_kernels, strip))
-    packed = pl.pallas_call(
-        pack_body,
-        out_shape=jax.ShapeDtypeStruct((320, 128), BF),
-        in_specs=[VMEM, pl.BlockSpec(memory_space=pltpu.SMEM), VMEM],
-        out_specs=VMEM,
-        scratch_shapes=[pltpu.VMEM((24, 40, 128), F32)],
-        compiler_params=pltpu.CompilerParams(vmem_limit_bytes=16 * 2**20),
-        cost_estimate=pl.CostEstimate(flops=10**6, bytes_accessed=3 * 10**5, transcendentals=0),
-        name="pack",
-    )(kernels.reshape(24, TAPS, TAPS), kernel_weights, strip)
     swap = [(0, 1), (1, 0)]
     other = lax.ppermute(packed, "kern", swap)
     outside = jnp.where(left, col == 0, col == n_col - 1)
@@ -324,7 +324,8 @@
     half = jnp.where(left, mask_full[:, :256], mask_full[:, 256:])
     gradient = (middle_rows + got_one + got_two) * half * (1.0 - half)
     mine = jnp.concatenate([resist, gradient], axis=0)
-    theirs = lax.ppermute(mine, "kern", swap)
+    mine = lax.reduce_precision(mine, 8, 7)
+    theirs = lax.ppermute(mine.astype(BF), "kern", swap).astype(F32)
     both = jnp.where(
         left, jnp.concatenate([mine, theirs], axis=1), jnp.concatenate([theirs, mine], axis=1)
     )

time: 39.2 us -> 34.7 us (0.89)
  local copies, waits for them, and re-layouts: 4.81 us -> 0.67 us
  waiting for transfers between devices: 5.97 us -> 5.46 us
    unnamed x8 -> x0, local copies, waits for them, and re-layouts: 3.16 us -> none
    optimization_barrier x1 -> x0, local copies, waits for them, and re-layouts: 0.97 us -> none  [per_device(): kernels, _ = lax.optimization_barrier((socs_kernels, strip))]
    ppermute x1, waiting for transfers between devices: 4.3 us -> 3.79 us  [per_device(): theirs = lax.ppermute(mine.astype(BF), 'kern', swap).astype(F32)]
    pallas_call x2 -> x1, Pallas kernels: 1.07 us -> 1.37 us  [per_device(): pl.pallas_call(start_body, out_shape=(pltpu.VMEM((ROWS, 128), BF), pltpu....]
  transfers between devices with their start and end apart: 7 -> 7, of which waited for: 3 -> 3; matrix products, arithmetic and copies ran while one was open for 3% -> 1% of each run, Pallas kernels for 10% -> 9%
where the time goes in v3:
time: 34.7 us; the launch traced here: 34.5 us
  starting transfers between devices  17.9 us (52%)
  Pallas kernels  9.58 us (28%)
  waiting for transfers between devices  5.46 us (16%)
  between operations  0.73 us (2%)
  local copies, waits for them, and re-layouts  0.67 us (2%)
    ppermute x1, starting transfers between devices, per_device(): other = lax.ppermute(packed, 'kern', swap)  6.5 us
    pallas_call x1, Pallas kernels, per_device(): pl.pallas_call(main_body, out_shape=(tile, tile, tile, tile, jax.ShapeDty...  5.1 us
    ppermute x1, starting transfers between devices, per_device(): strip_in = lax.ppermute(strip, ('col', 'kern'), to_right + to_left)  3.83 us
    ppermute x1, waiting for transfers between devices, per_device(): theirs = lax.ppermute(mine.astype(BF), 'kern', swap).astype(F32)  3.79 us
    ppermute x1, starting transfers between devices, per_device(): got_two = lax.ppermute(share_two, 'row', far)  2.04 us
    ppermute x1, starting transfers between devices, per_device(): two = lax.ppermute(own, 'row', far)  1.92 us
    pallas_call x1, Pallas kernels, per_device(): pl.pallas_call(rest_body, out_shape=tile, in_specs=[VMEM] * 3, out_specs=...  1.91 us
    ppermute x1, starting transfers between devices, per_device(): theirs = lax.ppermute(mine.astype(BF), 'kern', swap).astype(F32)  1.72 us
  transfers between devices with their start and end apart: 7, of which 3 were waited for; matrix products, arithmetic and copies ran while one was open for 1% of the time, Pallas kernels for 9%

profile of v3, /device:TPU:10, one launch (start us, length us, event | category | flops | bytes accessed | tf_op | source)
XLA Modules:
  0.0 34.5 jit_solution(11550668764010030289)
XLA Ops:
  0.6 1.4 %start.1 = (bf16[32,128]{1,0:T(8,128)(2,1)S(1)}, f32[32,512]{1,0:T(8,128)S(1)}, bf16[32,512]{1,0:T(8,128)(2,1)S(1)}, bf16[32,512]{1,0:T(8,128)(2,1)S(1)}, bf16[320,128]{1,0:T(8,128)(2,1)S(1)}) custom-call(s32[32,512]{1,0:T(8,128)} %levels.1, f32[32,512]{1,0:T(8,128)} %offset.1, s32[32,512]{1,0:T(8,128)} %bits.1, bf16[12,35,2,35]{3,2,1,0:T(2,128)(2,1)} %bitcast.1, ...), custom_call_target="tpu_custom_call" | custom-call | tf_op jit(solution)/shard_map/start/pallas_call | solution.py:237
  2.0 3.8 %collective-permute-start = (bf16[32,128]{1,0:T(8,128)(2,1)S(1)}, bf16[32,128]{1,0:T(8,128)(2,1)S(1)}, u32[]{:S(2)}, u32[]{:S(2)}) collective-permute-start(bf16[32,128]{1,0:T(8,128)(2,1)S(1)} %get-tuple-element.15), channel_id=1, source_target_pairs={{0,2},{2,4},{4,6},{6,8},{8,10},{10,12},{12,14},{14,16},{16,18},{18... | collective-permute-start | bytes 24584 | tf_op jit(solution)/shard_map/ppermute | solution.py:262
  5.8 6.5 %collective-permute-start.3 = (bf16[320,128]{1,0:T(8,128)(2,1)S(1)}, bf16[320,128]{1,0:T(8,128)(2,1)S(1)}, u32[]{:S(2)}, u32[]{:S(2)}) collective-permute-start(bf16[320,128]{1,0:T(8,128)(2,1)S(1)} %get-tuple-element.18.mine), channel_id=1, source_target_pairs={{0,1},{1,0},{2,3},{3,2},{4,5},{5,4},{6,7},{7,6},{8,9},{9,8},{10,11... | collective-permute-start | bytes 245768 | tf_op jit(solution)/shard_map/ppermute | solution.py:264
  12.4 0.0 collective-permute-done
  12.4 0.1 slice_select_fusion
  12.5 0.1 fusion.1
  12.6 1.9 %collective-permute-start.2 = (bf16[32,512]{1,0:T(8,128)(2,1)S(1)}, bf16[32,512]{1,0:T(8,128)(2,1)S(1)}, u32[]{:S(2)}, u32[]{:S(2)}) collective-permute-start(bf16[32,512]{1,0:T(8,128)(2,1)S(1)} %get-tuple-element.37.own), channel_id=1, source_target_pairs={{32,64},{64,32},{96,128},{128,96},{160,192},{192,160},{33,65},{65,... | collective-permute-start | bytes 98312 | tf_op jit(solution)/shard_map/ppermute | solution.py:282
  14.5 1.7 %collective-permute-start.1 = (bf16[32,512]{1,0:T(8,128)(2,1)S(1)}, bf16[32,512]{1,0:T(8,128)(2,1)S(1)}, u32[]{:S(2)}, u32[]{:S(2)}) collective-permute-start(bf16[32,512]{1,0:T(8,128)(2,1)S(1)} %get-tuple-element.37.own), channel_id=1, source_target_pairs={{0,32},{32,0},{64,96},{96,64},{128,160},{160,128},{192,224},{224,1... | collective-permute-start | bytes 98312 | tf_op jit(solution)/shard_map/ppermute | solution.py:281
  16.2 0.0 collective-permute-done.3.theirs
  16.2 1.2 %taps.1 = (bf16[384,1792]{1,0:T(8,128)(2,1)S(1)}, bf16[320,2304]{1,0:T(8,128)(2,1)S(1)}, f32[48,384]{1,0:T(8,128)S(1)}) custom-call(bf16[320,128]{1,0:T(8,128)(2,1)S(1)} %get-tuple-element.18.mine, bf16[320,128]{1,0:T(8,128)(2,1)S(1)} %collective-permute-done.3.theirs), custom_call_target="tpu_custom_call" | custom-call | flops 400000000 | bytes 4000000 | tf_op jit(solution)/shard_map/taps/pallas_call | solution.py:283
  17.4 0.4 %collective-permute-done.2.two = bf16[32,512]{1,0:T(8,128)(2,1)S(1)} collective-permute-done((bf16[32,512]{1,0:T(8,128)(2,1)S(1)}, bf16[32,512]{1,0:T(8,128)(2,1)S(1)}, u32[]{:S(2)}, u32[]{:S(2)}) %collective-permute-start.2) | collective-permute-done | bytes 32800 | tf_op jit(solution)/shard_map/ppermute | solution.py:282
  17.8 0.0 collective-permute-done.1.one
  17.8 5.1 %fields.1 = (f32[32,256]{1,0:T(8,128)S(1)}, f32[32,256]{1,0:T(8,128)S(1)}, f32[32,256]{1,0:T(8,128)S(1)}, f32[32,256]{1,0:T(8,128)S(1)}, bf16[1536,384]{1,0:T(8,128)(2,1)S(1)}) custom-call(bf16[32,512]{1,0:T(8,128)(2,1)S(1)} %collective-permute-done.1.one, bf16[32,512]{1,0:T(8,128)(2,1)S(1)} %get-tuple-element.37.own, ...), custom_call_target="tpu_custom_call" | custom-call | flops 6000000000 | bytes 6000000 | tf_op jit(solution)/shard_map/fields/pallas_call | solution.py:298
  22.9 0.2 collective-permute-start.4
  23.1 2.0 %collective-permute-start.5 = (f32[32,256]{1,0:T(8,128)S(1)}, f32[32,256]{1,0:T(8,128)S(1)}, u32[]{:S(2)}, u32[]{:S(2)}) collective-permute-start(f32[32,256]{1,0:T(8,128)S(1)} %get-tuple-element.26), channel_id=1, source_target_pairs={{32,64},{64,32},{96,128},{128,96},{160,192},{192,160},{33,65},{65,... | collective-permute-start | bytes 98312 | tf_op jit(solution)/shard_map/ppermute | solution.py:314
  25.2 1.9 %inner.1 = f32[32,256]{1,0:T(8,128)S(1)} custom-call(bf16[320,2304]{1,0:T(8,128)(2,1)S(1)} %get-tuple-element.21.adj, bf16[1536,384]{1,0:T(8,128)(2,1)S(1)} %get-tuple-element.23.charge, f32[32,256]{1,0:T(8,128)S(1)} %get-tuple-element.24.some), custom_call_target="tpu_custom_call" | custom-call | flops 2000000000 | bytes 3000000 | tf_op jit(solution)/shard_map/inner/pallas_call | solution.py:315
  27.1 0.0 collective-permute-done.4
  27.1 1.3 %collective-permute-done.5 = f32[32,256]{1,0:T(8,128)S(1)} collective-permute-done((f32[32,256]{1,0:T(8,128)S(1)}, f32[32,256]{1,0:T(8,128)S(1)}, u32[]{:S(2)}, u32[]{:S(2)}) %collective-permute-start.5) | collective-permute-done | bytes 32800 | tf_op jit(solution)/shard_map/ppermute | solution.py:314
  28.4 1.7 %collective-permute-start.6 = (bf16[64,256]{1,0:T(8,128)(2,1)S(1)}, bf16[64,256]{1,0:T(8,128)(2,1)S(1)}, u32[]{:S(2)}, u32[]{:S(2)}) collective-permute-start(bf16[64,256]{1,0:T(8,128)(2,1)S(1)} %get-tuple-element.31), channel_id=1, source_target_pairs={{0,1},{1,0},{2,3},{3,2},{4,5},{5,4},{6,7},{7,6},{8,9},{9,8},{10,11... | collective-permute-start | bytes 98312 | tf_op jit(solution)/shard_map/ppermute | solution.py:328
  30.1 3.8 %collective-permute-done.6 = bf16[64,256]{1,0:T(8,128)(2,1)S(1)} collective-permute-done((bf16[64,256]{1,0:T(8,128)(2,1)S(1)}, bf16[64,256]{1,0:T(8,128)(2,1)S(1)}, u32[]{:S(2)}, u32[]{:S(2)}) %collective-permute-start.6) | collective-permute-done | bytes 32800 | tf_op jit(solution)/shard_map/ppermute | solution.py:328
  33.9 0.7 %fusion.5 = (f32[32,512]{1,0:T(8,128)}, f32[32,512]{1,0:T(8,128)}) fusion(f32[64,512]{1,0:T(8,128)S(1)} %maximum_select_fusion), kind=kLoop, calls=%fused_computation.14 | loop fusion | bytes 262144 | tf_op jit(solution)/shard_map/slice | solution.py:332
  (6 shorter events, 0.1 us)
Async XLA Ops:
  2.0 10.4 %collective-permute-start = (bf16[32,128]{1,0:T(8,128)(2,1)S(1)}, bf16[32,128]{1,0:T(8,128)(2,1)S(1)}, u32[]{:S(2)}, u32[]{:S(2)}) collective-permute-start(bf16[32,128]{1,0:T(8,128)(2,1)S(1)} %get-tuple-element.15), channel_id=1, source_target_pairs={{0,2},{2,4},{4,6},{6,8},{8,10},{10,12},{12,14},{14,16},{16,18},{18... | collective-permute-start | bytes 24584 | tf_op jit(solution)/shard_map/ppermute | solution.py:262
  5.8 10.3 %collective-permute-start.3 = (bf16[320,128]{1,0:T(8,128)(2,1)S(1)}, bf16[320,128]{1,0:T(8,128)(2,1)S(1)}, u32[]{:S(2)}, u32[]{:S(2)}) collective-permute-start(bf16[320,128]{1,0:T(8,128)(2,1)S(1)} %get-tuple-element.18.mine), channel_id=1, source_target_pairs={{0,1},{1,0},{2,3},{3,2},{4,5},{5,4},{6,7},{7,6},{8,9},{9,8},{10,11... | collective-permute-start | bytes 245768 | tf_op jit(solution)/shard_map/ppermute | solution.py:264
  12.6 5.2 %collective-permute-start.2 = (bf16[32,512]{1,0:T(8,128)(2,1)S(1)}, bf16[32,512]{1,0:T(8,128)(2,1)S(1)}, u32[]{:S(2)}, u32[]{:S(2)}) collective-permute-start(bf16[32,512]{1,0:T(8,128)(2,1)S(1)} %get-tuple-element.37.own), channel_id=1, source_target_pairs={{32,64},{64,32},{96,128},{128,96},{160,192},{192,160},{33,65},{65,... | collective-permute-start | bytes 98312 | tf_op jit(solution)/shard_map/ppermute | solution.py:282
  14.5 3.3 %collective-permute-start.1 = (bf16[32,512]{1,0:T(8,128)(2,1)S(1)}, bf16[32,512]{1,0:T(8,128)(2,1)S(1)}, u32[]{:S(2)}, u32[]{:S(2)}) collective-permute-start(bf16[32,512]{1,0:T(8,128)(2,1)S(1)} %get-tuple-element.37.own), channel_id=1, source_target_pairs={{0,32},{32,0},{64,96},{96,64},{128,160},{160,128},{192,224},{224,1... | collective-permute-start | bytes 98312 | tf_op jit(solution)/shard_map/ppermute | solution.py:281
  22.9 4.2 %collective-permute-start.4 = (f32[32,256]{1,0:T(8,128)S(1)}, f32[32,256]{1,0:T(8,128)S(1)}, u32[]{:S(2)}, u32[]{:S(2)}) collective-permute-start(f32[32,256]{1,0:T(8,128)S(1)} %get-tuple-element.25), channel_id=1, source_target_pairs={{0,32},{32,0},{64,96},{96,64},{128,160},{160,128},{192,224},{224,1... | collective-permute-start | bytes 98312 | tf_op jit(solution)/shard_map/ppermute | solution.py:313
  23.1 5.2 %collective-permute-start.5 = (f32[32,256]{1,0:T(8,128)S(1)}, f32[32,256]{1,0:T(8,128)S(1)}, u32[]{:S(2)}, u32[]{:S(2)}) collective-permute-start(f32[32,256]{1,0:T(8,128)S(1)} %get-tuple-element.26), channel_id=1, source_target_pairs={{32,64},{64,32},{96,128},{128,96},{160,192},{192,160},{33,65},{65,... | collective-permute-start | bytes 98312 | tf_op jit(solution)/shard_map/ppermute | solution.py:314
  28.4 5.5 %collective-permute-start.6 = (bf16[64,256]{1,0:T(8,128)(2,1)S(1)}, bf16[64,256]{1,0:T(8,128)(2,1)S(1)}, u32[]{:S(2)}, u32[]{:S(2)}) collective-permute-start(bf16[64,256]{1,0:T(8,128)(2,1)S(1)} %get-tuple-element.31), channel_id=1, source_target_pairs={{0,1},{1,0},{2,3},{3,2},{4,5},{5,4},{6,7},{7,6},{8,9},{9,8},{10,11... | collective-permute-start | bytes 98312 | tf_op jit(solution)/shard_map/ppermute | solution.py:328

commit v4 on v3

--- a/solution.py
+++ b/solution.py
@@ -11,13 +11,15 @@
 TAPS = 35
 MARGIN = 17
 SLOT = 40
+STEP = 36
 BLOCK = 8
 ROWS = 32
 CHANNELS = 48
-FWD_K = 1792
+FWD_K = 1536
 ADJ_K = 2304
 LEAD = 6
 WIDE = 384
+IMAGE = 17 * 4 * STEP
 START_VMEM = 58 * 2**20
 BF = jnp.bfloat16
 F32 = jnp.float32
@@ -96,7 +98,55 @@
     return out
 
 
-def taps_body(mine, theirs, fwd, adj, wgt, plain, flipped):
+def turn(line, count, shift):
+    line = jnp.broadcast_to(line, (count, line.shape[1]))
+    return pltpu.roll(line, shift, 1, stride=1, stride_axis=0)
+
+
+def spread(rows, image, first, last):
+    early = lax.broadcasted_iota(jnp.int32, (8, 256), 0) < 4
+    for n in range(first, last):
+        parts = []
+        for r in (4 * n, 4 * n + 2):
+            a, b = rows[r : r + 1, :WIDE], rows[r + 1 : r + 2, :WIDE]
+            parts.append(turn(a, 32, 0)[:, 128:])
+            mixed = pltpu.roll(turn(b, 8, 0)[:, 128:], 4, 0)
+            parts.append(jnp.where(early, turn(a, 8, 32)[:, 128:], mixed))
+            parts.append(turn(b, 32, 4)[:, 128:])
+        image[144 * n : 144 * n + 144, :] = jnp.concatenate(parts, axis=0).astype(BF)
+
+
+def spread_ends(rows, side, lines, ends):
+    low = lax.broadcasted_iota(jnp.int32, (24, 128), 1) < 64
+    side[...] = pltpu.roll(rows[:, 256:], 192, 1)[:, :128]
+    for e in range(2):
+        moved = [side[pl.ds(8 * j + e, 24, stride=2), :] for j in range(4)]
+        for n in range(5):
+            shift = 8 * n - 4 * e
+            for t in range(2):
+                one = pltpu.roll(moved[2 * t], (shift - 56) % 128, 1)
+                two = pltpu.roll(moved[2 * t + 1], (shift + 8) % 128, 1)
+                at = 24 * (5 * e + n)
+                lines[at : at + 24, 128 * t : 128 * t + 128] = jnp.where(low, one, two)
+    early = lax.broadcasted_iota(jnp.int32, (8, 128), 0) < 4
+    for t in range(2):
+        lanes = slice(128 * t, 128 * t + 128)
+        parts = []
+        for c in range(21):
+            get = lambda e, n: turn(lines[24 * (5 * e + n) + c : 24 * (5 * e + n) + c + 1, lanes], 8, 0)
+            parts += [get(0, n) for n in range(4)]
+            parts.append(jnp.where(early, get(0, 4), get(1, 0)))
+            parts += [get(1, n) for n in range(1, 5)]
+            if c % 2:
+                ends[72 * (c - 1) : 72 * (c + 1), lanes] = jnp.concatenate(parts, axis=0).astype(BF)
+                parts = []
+        parts.append(jnp.zeros((24, 128), F32))
+        ends[1440:1536, lanes] = jnp.concatenate(parts, axis=0).astype(BF)
+
+
+def taps_body(mine, theirs, own, fwd, adj, wgt, image, plain, flipped, rows):
+    rows[17:49, :] = own[...].astype(F32)
+    spread(rows, image, 5, 12)
     row = lax.broadcasted_iota(jnp.int32, (128, 128), 0)
     column = lax.broadcasted_iota(jnp.int32, (128, 128), 1)
     group = jnp.where(row >= 80, 2, jnp.where(row >= 40, 1, 0))
@@ -114,25 +164,25 @@
 
     parts = (pick(plain, 0) + pick(plain, 1)) + pick(plain, 2)
     for i in range(3):
-        wgt[16 * i : 16 * i + 16, :] = jnp.broadcast_to(parts[:, 120 + i : 121 + i], (16, WIDE))
+        wgt[16 * i : 16 * i + 16, :] = jnp.broadcast_to(parts[:, 120 + i : 121 + i], (16, 256))
     lane = lax.broadcasted_iota(jnp.int32, (16, 128), 1)
     empty = jnp.zeros((16, 128), BF)
     for i in range(3):
-        tiles = [None] * 11
+        tiles = [None] * 10
         for a in range(TAPS):
-            first, off = divmod(SLOT * a, 128)
+            first, off = divmod(STEP * a, 128)
             turned = pick(flipped, a)
             if (off - SLOT * i) % 128:
                 turned = pltpu.roll(turned, (off - SLOT * i) % 128, 1)
-            inside = min(SLOT, 128 - off)
+            inside = min(STEP, 128 - off)
             piece = jnp.where((lane >= off) & (lane < off + inside), turned, 0.0)
             tiles[first] = piece if tiles[first] is None else tiles[first] + piece
-            if inside < SLOT:
-                piece = jnp.where(lane < SLOT - inside, turned, 0.0)
+            if inside < STEP:
+                piece = jnp.where(lane < STEP - inside, turned, 0.0)
                 tiles[first + 1] = piece
         for x in range(BLOCK):
             top = 128 * i + 16 * x
-            for n, tile in enumerate(shifted(tiles, SLOT * x, 14, lane)):
+            for n, tile in enumerate(shifted(tiles, STEP * x, 12, lane)):
                 fwd[top : top + 16, 128 * n : 128 * n + 128] = (
                     empty if tile is None else tile.astype(BF)
                 )
@@ -156,12 +206,12 @@
                 adj[SLOT * x : SLOT * (x + 2), at : at + 128] = jnp.concatenate(both, axis=0).astype(BF)
 
 
-def share(adj, charge, j):
+def share(adj, charge, j, count=BLOCK):
     low = max(0, 40 - 8 * j)
     high = min(48, 72 - 8 * j)
     first = low - 40 + 8 * j
     return jnp.dot(
-        adj[:, 48 * low : 48 * high],
+        adj[: SLOT * count, 48 * low : 48 * high],
         charge[48 * first : 48 * (first + high - low), :],
         preferred_element_type=F32,
     )
@@ -173,58 +223,77 @@
     return pltpu.roll(line, WIDE - 34, 1)[:, :256]
 
 
-def main_body(one, own, two, tgt, wgt, fwd, adj, res_out, one_out, two_out, some_out, charge, rows, image, up_out, dn_out):
+def main_body(one, own, two, tgt, wgt, fwd, adj, image_in, res_out, one_out, two_out, some_out, charge,
+              image, rows, side, lines, ends, up_out, dn_out):
+    del image_in
     even = lax.rem(lax.axis_index("row"), 2) == 0
     below = one[...].astype(F32)
     above = two[...].astype(F32)
-    rows[0:32, :] = jnp.where(even, above, below)
-    rows[32:64, :] = own[...].astype(F32)
-    rows[64:96, :] = jnp.where(even, below, above)
-    image[2640:2752, :] = jnp.zeros((112, WIDE), BF)
-    for p in range(33):
-        parts = []
-        for i in range(2):
-            line = jnp.broadcast_to(rows[15 + 2 * p + i : 16 + 2 * p + i, :], (SLOT, 512))
-            parts.append(pltpu.roll(line, 0, 1, stride=1, stride_axis=0)[:, 128:])
-        image[80 * p : 80 * p + 80, :] = jnp.concatenate(parts, axis=0).astype(BF)
-    weight = wgt[...].reshape(3, 1, 16, WIDE)
-    goal = pltpu.roll(tgt[...].astype(F32), 512 - 111, 1)[:, :WIDE]
-    for j in range(4):
-        fields = jnp.dot(fwd[...], image[320 * j : 320 * j + FWD_K, :], preferred_element_type=F32)
-        fields = fields.reshape(3, BLOCK, 16, WIDE)
+    rows[0:17, :] = jnp.where(even, above, below)[15:32]
+    rows[17:49, :] = own[...].astype(F32)
+    rows[49:66, :] = jnp.where(even, below, above)[0:17]
+    rows[66:72, :] = jnp.zeros((6, 512), F32)
+    spread(rows, image, 0, 5)
+    spread(rows, image, 12, 17)
+    spread_ends(rows, side, lines, ends)
+    weight = wgt[...].reshape(3, 1, 16, 256)
+    target = tgt[...].astype(F32)
+    goal = pltpu.roll(target, 512 - 111, 1)[:, :256]
+    low = lax.broadcasted_iota(jnp.int32, (8, 128), 1) < 64
+    late = lax.broadcasted_iota(jnp.int32, (8, 128), 1) >= 111
+
+    def tail(j):
+        return pltpu.roll(target[8 * j : 8 * j + 8, 256:], (64 * (j % 2) - 103) % 256, 1)[:, :128]
+
+    goal_ends = [jnp.where(low, tail(0), tail(1)), jnp.where(low, tail(2), tail(3))]
+
+    def respond(pixels, want):
+        fields = jnp.dot(fwd[...], pixels, preferred_element_type=F32)
+        fields = fields.reshape(3, BLOCK, 16, 256)
         squares = weight * fields * fields
         intensity = jnp.sum((squares[0] + squares[1]) + squares[2], axis=1)
         resist = jax.nn.sigmoid(STEEP * (intensity - THRESHOLD))
-        want = goal[8 * j : 8 * j + 8]
         slope = GAIN * (resist - want) * resist * (1.0 - resist)
         slope = jnp.where(want > 1.5, 0.0, slope)
         scaled = (2.0 * weight) * slope[None, :, None, :] * fields
-        charge[384 * j : 384 * j + 384, :] = scaled.reshape(384, WIDE).astype(BF)
-        res_out[8 * j : 8 * j + 8, :] = pltpu.roll(resist, WIDE - MARGIN, 1)[:, :256]
+        return resist, scaled.reshape(384, 256)
+
+    resist_ends, scaled = respond(ends[...], jnp.concatenate(goal_ends, axis=1))
+    for j in range(4):
+        tile = scaled[:, 128 * (j // 2) : 128 * (j // 2) + 128]
+        tile = pltpu.roll(tile, 120 - 64 * (j % 2), 1)
+        charge[384 * j : 384 * j + 384, 256:] = tile.astype(BF)
+    for j in range(4):
+        resist, scaled = respond(image[288 * j : 288 * j + FWD_K, :], goal[8 * j : 8 * j + 8])
+        charge[384 * j : 384 * j + 384, :256] = scaled.astype(BF)
+        resist = pltpu.roll(resist, 256 - MARGIN, 1)
+        end = resist_ends[:, 128 * (j // 2) : 128 * (j // 2) + 128]
+        end = pltpu.roll(end, (103 - 64 * (j % 2)) % 128, 1)
+        res_out[8 * j : 8 * j + 8, :128] = resist[:, :128]
+        res_out[8 * j : 8 * j + 8, 128:] = jnp.where(late, end, resist[:, 128:])
     up_out[0:15, :] = jnp.zeros((15, 256), F32)
     dn_out[17:32, :] = jnp.zeros((15, 256), F32)
-    for j in (0, 1, 2, 6, 7, 8):
+    for j, count in ((0, 8), (1, 8), (2, 1), (6, 8), (7, 8), (8, 2)):
+        part = share(adj, charge, j, count)
+        for i in range(count):
+            x = 8 * j + i - MARGIN
+            if x < 0:
+                up_out[ROWS + x : ROWS + x + 1, :] = fold(part, i)
+            elif x < ROWS:
+                some_out[...] = jnp.broadcast_to(fold(part, i), (8, 256))
+            else:
+                dn_out[x - ROWS : x - ROWS + 1, :] = fold(part, i)
+    one_out[...] = jnp.where(even, dn_out[...], up_out[...])
+    two_out[...] = jnp.where(even, up_out[...], dn_out[...])
+
+
+def rest_body(adj, charge, some, mid_out):
+    mid_out[31:32, :] = some[0:1, :]
+    for j in (2, 3, 4, 5):
         part = share(adj, charge, j)
         for i in range(BLOCK):
             x = 8 * j + i - MARGIN
-            if x < 0:
-                up_out[ROWS + x : ROWS + x + 1, :] = fold(part, i)
-            elif ROWS <= x <= ROWS + MARGIN - 1:
-                dn_out[x - ROWS : x - ROWS + 1, :] = fold(part, i)
-            elif 0 <= x < ROWS:
-                some_out[x : x + 1, :] = fold(part, i)
-    one_out[...] = jnp.where(even, dn_out[...], up_out[...])
-    two_out[...] = jnp.where(even, up_out[...], dn_out[...])
-
-
-def rest_body(adj, charge, some, mid_out):
-    mid_out[0:7, :] = some[0:7, :]
-    mid_out[31:32, :] = some[31:32, :]
-    for j in (3, 4, 5):
-        part = share(adj, charge, j)
-        for i in range(BLOCK):
-            x = 8 * j + i - MARGIN
-            if 0 <= x < ROWS:
+            if x >= 0:
                 mid_out[x : x + 1, :] = fold(part, i)
 
 
@@ -280,36 +349,51 @@
     far = [(i, ((i + 1) ^ 1) - 1) for i in range(1, n_row - 1)]
     one = lax.ppermute(own, "row", near)
     two = lax.ppermute(own, "row", far)
-    fwd, adj, weights = pl.pallas_call(
+    fwd, adj, weights, image = pl.pallas_call(
         taps_body,
         out_shape=(
             jax.ShapeDtypeStruct((384, FWD_K), BF),
             jax.ShapeDtypeStruct((SLOT * BLOCK, ADJ_K), BF),
-            jax.ShapeDtypeStruct((CHANNELS, WIDE), F32),
+            jax.ShapeDtypeStruct((CHANNELS, 256), F32),
+            jax.ShapeDtypeStruct((IMAGE, 256), BF),
         ),
-        in_specs=[VMEM] * 2,
-        out_specs=(VMEM,) * 3,
-        scratch_shapes=[pltpu.VMEM((640, 128), F32), pltpu.VMEM((640, 128), F32)],
+        in_specs=[VMEM] * 3,
+        out_specs=(VMEM,) * 4,
+        scratch_shapes=[
+            pltpu.VMEM((640, 128), F32),
+            pltpu.VMEM((640, 128), F32),
+            pltpu.VMEM((56, 512), F32),
+        ],
         compiler_params=pltpu.CompilerParams(vmem_limit_bytes=16 * 2**20),
         cost_estimate=pl.CostEstimate(flops=4 * 10**8, bytes_accessed=4 * 10**6, transcendentals=0),
         name="taps",
-    )(packed, other)
+    )(packed, other, own)
     tile = jax.ShapeDtypeStruct((ROWS, 256), F32)
-    resist, share_one, share_two, some, charge = pl.pallas_call(
+    resist, share_one, share_two, some, charge, _ = pl.pallas_call(
         main_body,
-        out_shape=(tile, tile, tile, tile, jax.ShapeDtypeStruct((1536, WIDE), BF)),
-        in_specs=[VMEM] * 7,
-        out_specs=(VMEM,) * 5,
+        out_shape=(
+            tile,
+            tile,
+            tile,
+            jax.ShapeDtypeStruct((8, 256), F32),
+            jax.ShapeDtypeStruct((1536, WIDE), BF),
+            jax.ShapeDtypeStruct((IMAGE, 256), BF),
+        ),
+        input_output_aliases={7: 5},
+        in_specs=[VMEM] * 8,
+        out_specs=(VMEM,) * 6,
         scratch_shapes=[
-            pltpu.VMEM((96, 512), F32),
-            pltpu.VMEM((2752, WIDE), BF),
+            pltpu.VMEM((72, 512), F32),
+            pltpu.VMEM((72, 128), F32),
+            pltpu.VMEM((240, 256), F32),
+            pltpu.VMEM((FWD_K, 256), BF),
             pltpu.VMEM((ROWS, 256), F32),
             pltpu.VMEM((ROWS, 256), F32),
         ],
         compiler_params=pltpu.CompilerParams(vmem_limit_bytes=24 * 2**20),
         cost_estimate=pl.CostEstimate(flops=6 * 10**9, bytes_accessed=6 * 10**6, transcendentals=0),
         name="fields",
-    )(one, own, two, goal, weights, fwd, adj)
+    )(one, own, two, goal, weights, fwd, adj, image)
     got_one = lax.ppermute(share_one, "row", near)
     got_two = lax.ppermute(share_two, "row", far)
     middle_rows = pl.pallas_call(

time: 34.7 us -> 33.4 us (0.963)
  waiting for transfers between devices: 5.46 us -> 4.56 us
  Pallas kernels: 9.58 us -> 8.82 us
  starting transfers between devices: 17.9 us -> 18.3 us
    pallas_call x1, Pallas kernels: 5.1 us -> 3.81 us  [per_device(): pl.pallas_call(main_body, out_shape=(tile, tile, tile, jax.ShapeDtypeStru...]
    ppermute x1, waiting for transfers between devices: 1.26 us -> 0.71 us  [per_device(): got_two = lax.ppermute(share_two, 'row', far)]
    pallas_call x1, Pallas kernels: 1.91 us -> 2.26 us  [per_device(): pl.pallas_call(rest_body, out_shape=tile, in_specs=[VMEM] * 3, out_specs=...]
  transfers between devices with their start and end apart: 7 -> 7, of which waited for: 3 -> 3; matrix products, arithmetic and copies ran while one was open for 1% -> 1% of each run, Pallas kernels for 9% -> 11%
where the time goes in v4:
time: 33.4 us; the launch traced here: 33.3 us
  starting transfers between devices  18.3 us (55%)
  Pallas kernels  8.82 us (26%)
  waiting for transfers between devices  4.56 us (14%)
  between operations  0.74 us (2%)
  local copies, waits for them, and re-layouts  0.67 us (2%)
    ppermute x1, starting transfers between devices, per_device(): other = lax.ppermute(packed, 'kern', swap)  6.5 us
    ppermute x1, starting transfers between devices, per_device(): strip_in = lax.ppermute(strip, ('col', 'kern'), to_right + to_left)  3.83 us
    pallas_call x1, Pallas kernels, per_device(): pl.pallas_call(main_body, out_shape=(tile, tile, tile, jax.ShapeDtypeStru...  3.81 us
    ppermute x1, waiting for transfers between devices, per_device(): theirs = lax.ppermute(mine.astype(BF), 'kern', swap).astype(F32)  3.6 us
    pallas_call x1, Pallas kernels, per_device(): pl.pallas_call(rest_body, out_shape=tile, in_specs=[VMEM] * 3, out_specs=...  2.26 us
    ppermute x1, starting transfers between devices, per_device(): got_two = lax.ppermute(share_two, 'row', far)  2.22 us
    ppermute x1, starting transfers between devices, per_device(): two = lax.ppermute(own, 'row', far)  1.92 us
    ppermute x1, starting transfers between devices, per_device(): theirs = lax.ppermute(mine.astype(BF), 'kern', swap).astype(F32)  1.9 us
  transfers between devices with their start and end apart: 7, of which 3 were waited for; matrix products, arithmetic and copies ran while one was open for 1% of the time, Pallas kernels for 11%

profile of v4, /device:TPU:10, one launch (start us, length us, event | category | flops | bytes accessed | tf_op | source)
XLA Modules:
  0.0 33.3 jit_solution(998955193317406974)
XLA Ops:
  0.6 1.4 %start.1 = (bf16[32,128]{1,0:T(8,128)(2,1)S(1)}, f32[32,512]{1,0:T(8,128)S(1)}, bf16[32,512]{1,0:T(8,128)(2,1)S(1)}, bf16[32,512]{1,0:T(8,128)(2,1)S(1)}, bf16[320,128]{1,0:T(8,128)(2,1)S(1)}) custom-call(s32[32,512]{1,0:T(8,128)} %levels.1, f32[32,512]{1,0:T(8,128)} %offset.1, s32[32,512]{1,0:T(8,128)} %bits.1, bf16[12,35,2,35]{3,2,1,0:T(2,128)(2,1)} %bitcast.1, ...), custom_call_target="tpu_custom_call" | custom-call | tf_op jit(solution)/shard_map/start/pallas_call | solution.py:306
  2.0 3.8 %collective-permute-start = (bf16[32,128]{1,0:T(8,128)(2,1)S(1)}, bf16[32,128]{1,0:T(8,128)(2,1)S(1)}, u32[]{:S(2)}, u32[]{:S(2)}) collective-permute-start(bf16[32,128]{1,0:T(8,128)(2,1)S(1)} %get-tuple-element.16), channel_id=1, source_target_pairs={{0,2},{2,4},{4,6},{6,8},{8,10},{10,12},{12,14},{14,16},{16,18},{18... | collective-permute-start | bytes 24584 | tf_op jit(solution)/shard_map/ppermute | solution.py:331
  5.8 6.5 %collective-permute-start.3 = (bf16[320,128]{1,0:T(8,128)(2,1)S(1)}, bf16[320,128]{1,0:T(8,128)(2,1)S(1)}, u32[]{:S(2)}, u32[]{:S(2)}) collective-permute-start(bf16[320,128]{1,0:T(8,128)(2,1)S(1)} %get-tuple-element.19.mine), channel_id=1, source_target_pairs={{0,1},{1,0},{2,3},{3,2},{4,5},{5,4},{6,7},{7,6},{8,9},{9,8},{10,11... | collective-permute-start | bytes 245768 | tf_op jit(solution)/shard_map/ppermute | solution.py:333
  12.4 0.0 collective-permute-done
  12.4 0.1 slice_select_fusion
  12.5 0.1 fusion.1
  12.6 1.9 %collective-permute-start.2 = (bf16[32,512]{1,0:T(8,128)(2,1)S(1)}, bf16[32,512]{1,0:T(8,128)(2,1)S(1)}, u32[]{:S(2)}, u32[]{:S(2)}) collective-permute-start(bf16[32,512]{1,0:T(8,128)(2,1)S(1)} %get-tuple-element.39.own), channel_id=1, source_target_pairs={{32,64},{64,32},{96,128},{128,96},{160,192},{192,160},{33,65},{65,... | collective-permute-start | bytes 98312 | tf_op jit(solution)/shard_map/ppermute | solution.py:351
  14.5 1.7 %collective-permute-start.1 = (bf16[32,512]{1,0:T(8,128)(2,1)S(1)}, bf16[32,512]{1,0:T(8,128)(2,1)S(1)}, u32[]{:S(2)}, u32[]{:S(2)}) collective-permute-start(bf16[32,512]{1,0:T(8,128)(2,1)S(1)} %get-tuple-element.39.own), channel_id=1, source_target_pairs={{0,32},{32,0},{64,96},{96,64},{128,160},{160,128},{192,224},{224,1... | collective-permute-start | bytes 98312 | tf_op jit(solution)/shard_map/ppermute | solution.py:350
  16.2 0.0 collective-permute-done.3.theirs
  16.2 1.4 %taps.1 = (bf16[384,1536]{1,0:T(8,128)(2,1)S(1)}, bf16[320,2304]{1,0:T(8,128)(2,1)S(1)}, f32[48,256]{1,0:T(8,128)S(1)}, bf16[2448,256]{1,0:T(8,128)(2,1)S(1)}) custom-call(bf16[320,128]{1,0:T(8,128)(2,1)S(1)} %get-tuple-element.19.mine, bf16[320,128]{1,0:T(8,128)(2,1)S(1)} %collective-permute-done.3.theirs, bf16[32,512]{1,0:T(8,128)(2,1)S(1)} %get-tuple-element.39.own), custom_call_target="tpu_custom_call" | custom-call | flops 400000000 | bytes 4000000 | tf_op jit(solution)/shard_map/taps/pallas_call | solution.py:352
  17.6 0.2 collective-permute-done.2.two
  17.8 0.0 collective-permute-done.1.one
  17.8 3.8 %fields.1 = (f32[32,256]{1,0:T(8,128)S(1)}, f32[32,256]{1,0:T(8,128)S(1)}, f32[32,256]{1,0:T(8,128)S(1)}, f32[8,256]{1,0:T(8,128)S(1)}, bf16[1536,384]{1,0:T(8,128)(2,1)S(1)}, /*index=5*/bf16[2448,256]{1,0:T(8,128)(2,1)S(1)}) custom-call(bf16[32,512]{1,0:T(8,128)(2,1)S(1)} %collective-permute-done.1.one, ...), custom_call_target="tpu_custom_call", output_to_operand_aliasing={{5}: (7, {})} | custom-call | flops 6000000000 | bytes 6000000 | tf_op jit(solution)/shard_map/fields/pallas_call | solution.py:372
  21.6 0.2 collective-permute-start.4
  21.8 2.2 %collective-permute-start.5 = (f32[32,256]{1,0:T(8,128)S(1)}, f32[32,256]{1,0:T(8,128)S(1)}, u32[]{:S(2)}, u32[]{:S(2)}) collective-permute-start(f32[32,256]{1,0:T(8,128)S(1)} %get-tuple-element.28), channel_id=1, source_target_pairs={{32,64},{64,32},{96,128},{128,96},{160,192},{192,160},{33,65},{65,... | collective-permute-start | bytes 98312 | tf_op jit(solution)/shard_map/ppermute | solution.py:398
  24.0 2.3 %inner.1 = f32[32,256]{1,0:T(8,128)S(1)} custom-call(bf16[320,2304]{1,0:T(8,128)(2,1)S(1)} %get-tuple-element.22.adj, bf16[1536,384]{1,0:T(8,128)(2,1)S(1)} %get-tuple-element.25.charge, f32[8,256]{1,0:T(8,128)S(1)} %get-tuple-element.26.some), custom_call_target="tpu_custom_call" | custom-call | flops 2000000000 | bytes 3000000 | tf_op jit(solution)/shard_map/inner/pallas_call | solution.py:399
  26.3 0.0 collective-permute-done.4
  26.3 0.7 %collective-permute-done.5 = f32[32,256]{1,0:T(8,128)S(1)} collective-permute-done((f32[32,256]{1,0:T(8,128)S(1)}, f32[32,256]{1,0:T(8,128)S(1)}, u32[]{:S(2)}, u32[]{:S(2)}) %collective-permute-start.5) | collective-permute-done | bytes 32800 | tf_op jit(solution)/shard_map/ppermute | solution.py:398
  27.1 1.9 %collective-permute-start.6 = (bf16[64,256]{1,0:T(8,128)(2,1)S(1)}, bf16[64,256]{1,0:T(8,128)(2,1)S(1)}, u32[]{:S(2)}, u32[]{:S(2)}) collective-permute-start(bf16[64,256]{1,0:T(8,128)(2,1)S(1)} %get-tuple-element.33), channel_id=1, source_target_pairs={{0,1},{1,0},{2,3},{3,2},{4,5},{5,4},{6,7},{7,6},{8,9},{9,8},{10,11... | collective-permute-start | bytes 98312 | tf_op jit(solution)/shard_map/ppermute | solution.py:412
  29.0 3.6 %collective-permute-done.6 = bf16[64,256]{1,0:T(8,128)(2,1)S(1)} collective-permute-done((bf16[64,256]{1,0:T(8,128)(2,1)S(1)}, bf16[64,256]{1,0:T(8,128)(2,1)S(1)}, u32[]{:S(2)}, u32[]{:S(2)}) %collective-permute-start.6) | collective-permute-done | bytes 32800 | tf_op jit(solution)/shard_map/ppermute | solution.py:412
  32.6 0.7 %fusion.5 = (f32[32,512]{1,0:T(8,128)}, f32[32,512]{1,0:T(8,128)}) fusion(f32[64,512]{1,0:T(8,128)S(1)} %maximum_select_fusion), kind=kLoop, calls=%fused_computation.14 | loop fusion | bytes 262144 | tf_op jit(solution)/shard_map/slice | solution.py:416
  (6 shorter events, 0.1 us)
Async XLA Ops:
  2.0 10.4 %collective-permute-start = (bf16[32,128]{1,0:T(8,128)(2,1)S(1)}, bf16[32,128]{1,0:T(8,128)(2,1)S(1)}, u32[]{:S(2)}, u32[]{:S(2)}) collective-permute-start(bf16[32,128]{1,0:T(8,128)(2,1)S(1)} %get-tuple-element.16), channel_id=1, source_target_pairs={{0,2},{2,4},{4,6},{6,8},{8,10},{10,12},{12,14},{14,16},{16,18},{18... | collective-permute-start | bytes 24584 | tf_op jit(solution)/shard_map/ppermute | solution.py:331
  5.8 10.3 %collective-permute-start.3 = (bf16[320,128]{1,0:T(8,128)(2,1)S(1)}, bf16[320,128]{1,0:T(8,128)(2,1)S(1)}, u32[]{:S(2)}, u32[]{:S(2)}) collective-permute-start(bf16[320,128]{1,0:T(8,128)(2,1)S(1)} %get-tuple-element.19.mine), channel_id=1, source_target_pairs={{0,1},{1,0},{2,3},{3,2},{4,5},{5,4},{6,7},{7,6},{8,9},{9,8},{10,11... | collective-permute-start | bytes 245768 | tf_op jit(solution)/shard_map/ppermute | solution.py:333
  12.6 5.2 %collective-permute-start.2 = (bf16[32,512]{1,0:T(8,128)(2,1)S(1)}, bf16[32,512]{1,0:T(8,128)(2,1)S(1)}, u32[]{:S(2)}, u32[]{:S(2)}) collective-permute-start(bf16[32,512]{1,0:T(8,128)(2,1)S(1)} %get-tuple-element.39.own), channel_id=1, source_target_pairs={{32,64},{64,32},{96,128},{128,96},{160,192},{192,160},{33,65},{65,... | collective-permute-start | bytes 98312 | tf_op jit(solution)/shard_map/ppermute | solution.py:351
  14.5 3.3 %collective-permute-start.1 = (bf16[32,512]{1,0:T(8,128)(2,1)S(1)}, bf16[32,512]{1,0:T(8,128)(2,1)S(1)}, u32[]{:S(2)}, u32[]{:S(2)}) collective-permute-start(bf16[32,512]{1,0:T(8,128)(2,1)S(1)} %get-tuple-element.39.own), channel_id=1, source_target_pairs={{0,32},{32,0},{64,96},{96,64},{128,160},{160,128},{192,224},{224,1... | collective-permute-start | bytes 98312 | tf_op jit(solution)/shard_map/ppermute | solution.py:350
  21.6 4.7 %collective-permute-start.4 = (f32[32,256]{1,0:T(8,128)S(1)}, f32[32,256]{1,0:T(8,128)S(1)}, u32[]{:S(2)}, u32[]{:S(2)}) collective-permute-start(f32[32,256]{1,0:T(8,128)S(1)} %get-tuple-element.27), channel_id=1, source_target_pairs={{0,32},{32,0},{64,96},{96,64},{128,160},{160,128},{192,224},{224,1... | collective-permute-start | bytes 98312 | tf_op jit(solution)/shard_map/ppermute | solution.py:397
  21.8 5.2 %collective-permute-start.5 = (f32[32,256]{1,0:T(8,128)S(1)}, f32[32,256]{1,0:T(8,128)S(1)}, u32[]{:S(2)}, u32[]{:S(2)}) collective-permute-start(f32[32,256]{1,0:T(8,128)S(1)} %get-tuple-element.28), channel_id=1, source_target_pairs={{32,64},{64,32},{96,128},{128,96},{160,192},{192,160},{33,65},{65,... | collective-permute-start | bytes 98312 | tf_op jit(solution)/shard_map/ppermute | solution.py:398
  27.1 5.5 %collective-permute-start.6 = (bf16[64,256]{1,0:T(8,128)(2,1)S(1)}, bf16[64,256]{1,0:T(8,128)(2,1)S(1)}, u32[]{:S(2)}, u32[]{:S(2)}) collective-permute-start(bf16[64,256]{1,0:T(8,128)(2,1)S(1)} %get-tuple-element.33), channel_id=1, source_target_pairs={{0,1},{1,0},{2,3},{3,2},{4,5},{5,4},{6,7},{7,6},{8,9},{9,8},{10,11... | collective-permute-start | bytes 98312 | tf_op jit(solution)/shard_map/ppermute | solution.py:412

commit v5 on v4

--- a/solution.py
+++ b/solution.py
@@ -27,14 +27,13 @@
 HBM = pl.BlockSpec(memory_space=pltpu.HBM)
 
 
-def start_body(levels, offset, bits, kernels, weights, strip, full, short, goal, packed,
-               levels_v, offset_v, bits_v, kernels_v, weights_v, lines, sems):
+def start_body(levels, offset, bits, kernels, weights, strip, full, short, goal, kernels_v, parts,
+               levels_v, offset_v, bits_v, weights_v, sems):
     sources = (kernels, weights, levels, offset, bits)
     targets = (kernels_v, weights_v, levels_v, offset_v, bits_v)
     moves = [pltpu.make_async_copy(a, b, sems.at[n]) for n, (a, b) in enumerate(zip(sources, targets))]
     for move in moves:
         move.start()
-    lines[...] = jnp.zeros((840, 128), F32)
     left = lax.axis_index("kern") == 0
     for move in moves[2:]:
         move.wait()
@@ -49,11 +48,9 @@
     strip[...] = jnp.where(left, ends, starts).astype(BF)
     for move in moves[:2]:
         move.wait()
-    for n in range(12):
-        lines[70 * n : 70 * n + 70, 0:TAPS] = kernels_v[n].astype(F32).reshape(70, TAPS)
     row = lax.broadcasted_iota(jnp.int32, (8, 128), 0)
     lane = lax.broadcasted_iota(jnp.int32, (8, 128), 1)
-    index = 4 * jnp.maximum(lane - 120, 0) + lax.div(row, 2)
+    index = 4 * jnp.maximum(lane - 120, 0) + lax.rem(row, 4)
     table = jnp.zeros((8, 128), F32)
     for n in range(12):
         table = jnp.where(index == n, weights_v[n], table)
@@ -61,19 +58,19 @@
     high = table.astype(BF).astype(F32)
     middle = (table - high).astype(BF).astype(F32)
     lower = table - high - middle
-    blank = jnp.zeros((SLOT - TAPS, 128), F32)
-    for g in range(8):
-        at = 70 * (g // 2) + g % 2
-        tile = lines[pl.ds(at, TAPS, stride=2), :]
-        tile = tile + pltpu.roll(lines[pl.ds(at + 280, TAPS, stride=2), :], 40, 1)
-        tile = tile + pltpu.roll(lines[pl.ds(at + 560, TAPS, stride=2), :], 80, 1)
-        tile = jnp.concatenate([tile, blank], axis=0)
-        extra = jnp.where(
-            row == 0, high[g : g + 1], jnp.where(row == 1, middle[g : g + 1], lower[g : g + 1])
-        )
-        extra = jnp.where(row < 3, extra, 0.0)
-        tile = jnp.concatenate([tile[:8] + extra, tile[8:]], axis=0)
-        packed[40 * g : 40 * g + 40, :] = tile.astype(BF)
+    parts[0:8, :] = high
+    parts[8:16, :] = middle
+    parts[16:24, :] = lower
+
+
+def pack_body(kernels, parts, packed, plane, lines):
+    plane[...] = jnp.zeros((72, 128), F32)
+    for n in range(12):
+        plane[0:70, 0:TAPS] = kernels[n].astype(F32).reshape(70, TAPS)
+        lines[pl.ds(280 * (n // 4) + n % 4, 70, stride=4), :] = plane[0:70, :]
+    lines[0:24, :] = lines[0:24, :] + parts[...]
+    tile = lines[0:280, :] + pltpu.roll(lines[280:560, :], 40, 1) + pltpu.roll(lines[560:840, :], 80, 1)
+    packed[...] = tile.astype(BF)
 
 
 def shifted(tiles, shift, count, lane):
@@ -144,9 +141,12 @@
         ends[1440:1536, lanes] = jnp.concatenate(parts, axis=0).astype(BF)
 
 
-def taps_body(mine, theirs, own, fwd, adj, wgt, image, plain, flipped, rows):
+def own_body(own, image, rows):
     rows[17:49, :] = own[...].astype(F32)
     spread(rows, image, 5, 12)
+
+
+def taps_body(mine, theirs, fwd, adj, wgt, plain, flipped):
     row = lax.broadcasted_iota(jnp.int32, (128, 128), 0)
     column = lax.broadcasted_iota(jnp.int32, (128, 128), 1)
     group = jnp.where(row >= 80, 2, jnp.where(row >= 40, 1, 0))
@@ -154,12 +154,12 @@
     flip = flip.astype(F32).astype(BF)
     for p, source in enumerate((mine, theirs)):
         block = source[...]
-        plain[320 * p : 320 * p + 320, :] = block.astype(F32)
-        flipped[320 * p : 320 * p + 320, :] = jnp.dot(block, flip, preferred_element_type=F32)
+        plain[280 * p : 280 * p + 280, :] = block.astype(F32)
+        flipped[280 * p : 280 * p + 280, :] = jnp.dot(block, flip, preferred_element_type=F32)
 
     def pick(ref, a):
         return jnp.concatenate(
-            [ref[pl.ds(a, 8, stride=40), :], ref[pl.ds(320 + a, 8, stride=40), :]], axis=0
+            [ref[8 * a : 8 * a + 8, :], ref[280 + 8 * a : 288 + 8 * a, :]], axis=0
         )
 
     parts = (pick(plain, 0) + pick(plain, 1)) + pick(plain, 2)
@@ -303,24 +303,23 @@
     n_row, n_col = lax.axis_size("row"), lax.axis_size("col")
     left = kern == 0
     wide = lambda dtype: jax.ShapeDtypeStruct((ROWS, 512), dtype)
-    strip, mask_full, mask_bf, target, packed = pl.pallas_call(
+    strip, mask_full, mask_bf, target, kernels, parts = pl.pallas_call(
         start_body,
         out_shape=(
             pltpu.VMEM((ROWS, 128), BF),
             pltpu.VMEM((ROWS, 512), F32),
             pltpu.VMEM((ROWS, 512), BF),
             pltpu.VMEM((ROWS, 512), BF),
-            pltpu.VMEM((320, 128), BF),
+            pltpu.VMEM((12, TAPS, 2, TAPS), BF),
+            pltpu.VMEM((24, 128), F32),
         ),
         in_specs=[HBM] * 5,
-        out_specs=(VMEM,) * 5,
+        out_specs=(VMEM,) * 6,
         scratch_shapes=[
             pltpu.VMEM((ROWS, 512), jnp.int32),
             pltpu.VMEM((ROWS, 512), F32),
             pltpu.VMEM((ROWS, 512), jnp.int32),
-            pltpu.VMEM((12, TAPS, 2, TAPS), BF),
             pltpu.SMEM((12,), F32),
-            pltpu.VMEM((840, 128), F32),
             pltpu.SemaphoreType.DMA((5,)),
         ],
         compiler_params=pltpu.CompilerParams(vmem_limit_bytes=START_VMEM),
@@ -329,6 +328,16 @@
     to_right = [(2 * c, 2 * c + 2) for c in range(n_col - 1)]
     to_left = [(2 * c + 3, 2 * c + 1) for c in range(n_col - 1)]
     strip_in = lax.ppermute(strip, ("col", "kern"), to_right + to_left)
+    packed = pl.pallas_call(
+        pack_body,
+        out_shape=jax.ShapeDtypeStruct((280, 128), BF),
+        in_specs=[VMEM] * 2,
+        out_specs=VMEM,
+        scratch_shapes=[pltpu.VMEM((72, 128), F32), pltpu.VMEM((840, 128), F32)],
+        compiler_params=pltpu.CompilerParams(vmem_limit_bytes=16 * 2**20),
+        cost_estimate=pl.CostEstimate(flops=10**6, bytes_accessed=3 * 10**5, transcendentals=0),
+        name="pack",
+    )(kernels, parts)
     swap = [(0, 1), (1, 0)]
     other = lax.ppermute(packed, "kern", swap)
     outside = jnp.where(left, col == 0, col == n_col - 1)
@@ -349,25 +358,33 @@
     far = [(i, ((i + 1) ^ 1) - 1) for i in range(1, n_row - 1)]
     one = lax.ppermute(own, "row", near)
     two = lax.ppermute(own, "row", far)
-    fwd, adj, weights, image = pl.pallas_call(
+    image = pl.pallas_call(
+        own_body,
+        out_shape=jax.ShapeDtypeStruct((IMAGE, 256), BF),
+        in_specs=[VMEM],
+        out_specs=VMEM,
+        scratch_shapes=[pltpu.VMEM((56, 512), F32)],
+        compiler_params=pltpu.CompilerParams(vmem_limit_bytes=16 * 2**20),
+        cost_estimate=pl.CostEstimate(flops=10**8, bytes_accessed=10**6, transcendentals=0),
+        name="own",
+    )(own)
+    fwd, adj, weights = pl.pallas_call(
         taps_body,
         out_shape=(
             jax.ShapeDtypeStruct((384, FWD_K), BF),
             jax.ShapeDtypeStruct((SLOT * BLOCK, ADJ_K), BF),
             jax.ShapeDtypeStruct((CHANNELS, 256), F32),
-            jax.ShapeDtypeStruct((IMAGE, 256), BF),
         ),
-        in_specs=[VMEM] * 3,
-        out_specs=(VMEM,) * 4,
+        in_specs=[VMEM] * 2,
+        out_specs=(VMEM,) * 3,
         scratch_shapes=[
-            pltpu.VMEM((640, 128), F32),
-            pltpu.VMEM((640, 128), F32),
-            pltpu.VMEM((56, 512), F32),
+            pltpu.VMEM((560, 128), F32),
+            pltpu.VMEM((560, 128), F32),
         ],
         compiler_params=pltpu.CompilerParams(vmem_limit_bytes=16 * 2**20),
         cost_estimate=pl.CostEstimate(flops=4 * 10**8, bytes_accessed=4 * 10**6, transcendentals=0),
         name="taps",
-    )(packed, other, own)
+    )(packed, other)
     tile = jax.ShapeDtypeStruct((ROWS, 256), F32)
     resist, share_one, share_two, some, charge, _ = pl.pallas_call(
         main_body,
@@ -394,8 +411,8 @@
         cost_estimate=pl.CostEstimate(flops=6 * 10**9, bytes_accessed=6 * 10**6, transcendentals=0),
         name="fields",
     )(one, own, two, goal, weights, fwd, adj, image)
+    got_two = lax.ppermute(share_two, "row", far)
     got_one = lax.ppermute(share_one, "row", near)
-    got_two = lax.ppermute(share_two, "row", far)
     middle_rows = pl.pallas_call(
         rest_body,
         out_shape=tile,

time: 33.4 us -> 33.6 us (level)
    pallas_call x0 -> x2, Pallas kernels: none -> 0.6 us  [the longest x1 0.3 us: per_device(): pl.pallas_call(pack_body, out_shape=jax.ShapeDtypeStruct((280, 128), BF),...]
    ppermute x1, starting transfers between devices: 1.9 us -> 1.55 us  [per_device(): theirs = lax.ppermute(mine.astype(BF), 'kern', swap).astype(F32)]
    ppermute x1, waiting for transfers between devices: 3.6 us -> 3.96 us  [per_device(): theirs = lax.ppermute(mine.astype(BF), 'kern', swap).astype(F32)]
  transfers between devices with their start and end apart: 7 -> 7, of which waited for: 3 -> 3; matrix products, arithmetic and copies ran while one was open for 1% -> 1% of each run, Pallas kernels for 11% -> 12%
where the time goes in v5:
time: 33.6 us; the launch traced here: 33.4 us
  starting transfers between devices  18 us (54%)
  Pallas kernels  8.97 us (27%)
  waiting for transfers between devices  4.79 us (14%)
  between operations  0.76 us (2%)
  local copies, waits for them, and re-layouts  0.67 us (2%)
    ppermute x1, starting transfers between devices, per_device(): other = lax.ppermute(packed, 'kern', swap)  6.5 us
    ppermute x1, waiting for transfers between devices, per_device(): theirs = lax.ppermute(mine.astype(BF), 'kern', swap).astype(F32)  3.96 us
    ppermute x1, starting transfers between devices, per_device(): strip_in = lax.ppermute(strip, ('col', 'kern'), to_right + to_left)  3.83 us
    pallas_call x1, Pallas kernels, per_device(): pl.pallas_call(main_body, out_shape=(tile, tile, tile, jax.ShapeDtypeStru...  3.81 us
    ppermute x1, starting transfers between devices, per_device(): got_two = lax.ppermute(share_two, 'row', far)  2.28 us
    pallas_call x1, Pallas kernels, per_device(): pl.pallas_call(rest_body, out_shape=tile, in_specs=[VMEM] * 3, out_specs=...  2.26 us
    ppermute x1, starting transfers between devices, per_device(): two = lax.ppermute(own, 'row', far)  1.92 us
    ppermute x1, starting transfers between devices, per_device(): one = lax.ppermute(own, 'row', near)  1.68 us
  transfers between devices with their start and end apart: 7, of which 3 were waited for; matrix products, arithmetic and copies ran while one was open for 1% of the time, Pallas kernels for 12%

profile of v5, /device:TPU:10, one launch (start us, length us, event | category | flops | bytes accessed | tf_op | source)
XLA Modules:
  0.0 33.4 jit_solution(12711786205526437548)
XLA Ops:
  0.6 1.2 %start.1 = (bf16[32,128]{1,0:T(8,128)(2,1)S(1)}, f32[32,512]{1,0:T(8,128)S(1)}, bf16[32,512]{1,0:T(8,128)(2,1)S(1)}, bf16[32,512]{1,0:T(8,128)(2,1)S(1)}, bf16[1...) custom-call(s32[32,512]{1,0:T(8,128)} %levels.1, f32[32,512]{1,0:T(8,128)} %offset.1, s32[32,512]{1,0:T(8,128)} %bits.1, ...), custom_call_target="tpu_custom_call" | custom-call | tf_op jit(solution)/shard_map/start/pallas_call | solution.py:306
  1.8 3.8 %collective-permute-start = (bf16[32,128]{1,0:T(8,128)(2,1)S(1)}, bf16[32,128]{1,0:T(8,128)(2,1)S(1)}, u32[]{:S(2)}, u32[]{:S(2)}) collective-permute-start(bf16[32,128]{1,0:T(8,128)(2,1)S(1)} %get-tuple-element.16), channel_id=1, source_target_pairs={{0,2},{2,4},{4,6},{6,8},{8,10},{10,12},{12,14},{14,16},{16,18},{18... | collective-permute-start | bytes 24584 | tf_op jit(solution)/shard_map/ppermute | solution.py:330
  5.6 0.3 pack.1.mine
  5.9 6.5 %collective-permute-start.3 = (bf16[280,128]{1,0:T(8,128)(2,1)S(1)}, bf16[280,128]{1,0:T(8,128)(2,1)S(1)}, u32[]{:S(2)}, u32[]{:S(2)}) collective-permute-start(bf16[280,128]{1,0:T(8,128)(2,1)S(1)} %pack.1.mine), channel_id=1, source_target_pairs={{0,1},{1,0},{2,3},{3,2},{4,5},{5,4},{6,7},{7,6},{8,9},{9,8},{10,11... | collective-permute-start | bytes 215048 | tf_op jit(solution)/shard_map/ppermute | solution.py:342
  12.5 0.0 collective-permute-done
  12.5 0.1 slice_select_fusion
  12.6 0.1 fusion.1
  12.7 1.9 %collective-permute-start.2 = (bf16[32,512]{1,0:T(8,128)(2,1)S(1)}, bf16[32,512]{1,0:T(8,128)(2,1)S(1)}, u32[]{:S(2)}, u32[]{:S(2)}) collective-permute-start(bf16[32,512]{1,0:T(8,128)(2,1)S(1)} %get-tuple-element.39.own), channel_id=1, source_target_pairs={{32,64},{64,32},{96,128},{128,96},{160,192},{192,160},{33,65},{65,... | collective-permute-start | bytes 98312 | tf_op jit(solution)/shard_map/ppermute | solution.py:360
  14.6 1.7 %collective-permute-start.1 = (bf16[32,512]{1,0:T(8,128)(2,1)S(1)}, bf16[32,512]{1,0:T(8,128)(2,1)S(1)}, u32[]{:S(2)}, u32[]{:S(2)}) collective-permute-start(bf16[32,512]{1,0:T(8,128)(2,1)S(1)} %get-tuple-element.39.own), channel_id=1, source_target_pairs={{0,32},{32,0},{64,96},{96,64},{128,160},{160,128},{192,224},{224,1... | collective-permute-start | bytes 98312 | tf_op jit(solution)/shard_map/ppermute | solution.py:359
  16.3 0.3 own.1.image_in
  16.6 0.0 collective-permute-done.3.theirs
  16.6 1.1 %taps.1 = (bf16[384,1536]{1,0:T(8,128)(2,1)S(1)}, bf16[320,2304]{1,0:T(8,128)(2,1)S(1)}, f32[48,256]{1,0:T(8,128)S(1)}) custom-call(bf16[280,128]{1,0:T(8,128)(2,1)S(1)} %pack.1.mine, bf16[280,128]{1,0:T(8,128)(2,1)S(1)} %collective-permute-done.3.theirs), custom_call_target="tpu_custom_call" | custom-call | flops 400000000 | bytes 4000000 | tf_op jit(solution)/shard_map/taps/pallas_call | solution.py:371
  17.7 0.2 collective-permute-done.2.two
  17.9 0.0 collective-permute-done.1.one
  17.9 3.8 %fields.1 = (f32[32,256]{1,0:T(8,128)S(1)}, f32[32,256]{1,0:T(8,128)S(1)}, f32[32,256]{1,0:T(8,128)S(1)}, f32[8,256]{1,0:T(8,128)S(1)}, bf16[1536,384]{1,0:T(8,128)(2,1)S(1)}, /*index=5*/bf16[2448,256]{1,0:T(8,128)(2,1)S(1)}) custom-call(bf16[32,512]{1,0:T(8,128)(2,1)S(1)} %collective-permute-done.1.one, ...), custom_call_target="tpu_custom_call", output_to_operand_aliasing={{5}: (7, {})} | custom-call | flops 6000000000 | bytes 6000000 | tf_op jit(solution)/shard_map/fields/pallas_call | solution.py:389
  21.7 0.2 collective-permute-start.4
  21.9 2.3 %collective-permute-start.5 = (f32[32,256]{1,0:T(8,128)S(1)}, f32[32,256]{1,0:T(8,128)S(1)}, u32[]{:S(2)}, u32[]{:S(2)}) collective-permute-start(f32[32,256]{1,0:T(8,128)S(1)} %get-tuple-element.28), channel_id=1, source_target_pairs={{32,64},{64,32},{96,128},{128,96},{160,192},{192,160},{33,65},{65,... | collective-permute-start | bytes 98312 | tf_op jit(solution)/shard_map/ppermute | solution.py:414
  24.2 2.3 %inner.1 = f32[32,256]{1,0:T(8,128)S(1)} custom-call(bf16[320,2304]{1,0:T(8,128)(2,1)S(1)} %get-tuple-element.23.adj, bf16[1536,384]{1,0:T(8,128)(2,1)S(1)} %get-tuple-element.25.charge, f32[8,256]{1,0:T(8,128)S(1)} %get-tuple-element.26.some), custom_call_target="tpu_custom_call" | custom-call | flops 2000000000 | bytes 3000000 | tf_op jit(solution)/shard_map/inner/pallas_call | solution.py:416
  26.5 0.0 collective-permute-done.4
  26.5 0.6 %collective-permute-done.5 = f32[32,256]{1,0:T(8,128)S(1)} collective-permute-done((f32[32,256]{1,0:T(8,128)S(1)}, f32[32,256]{1,0:T(8,128)S(1)}, u32[]{:S(2)}, u32[]{:S(2)}) %collective-permute-start.5) | collective-permute-done | bytes 32800 | tf_op jit(solution)/shard_map/ppermute | solution.py:414
  27.2 1.5 %collective-permute-start.6 = (bf16[64,256]{1,0:T(8,128)(2,1)S(1)}, bf16[64,256]{1,0:T(8,128)(2,1)S(1)}, u32[]{:S(2)}, u32[]{:S(2)}) collective-permute-start(bf16[64,256]{1,0:T(8,128)(2,1)S(1)} %get-tuple-element.33), channel_id=1, source_target_pairs={{0,1},{1,0},{2,3},{3,2},{4,5},{5,4},{6,7},{7,6},{8,9},{9,8},{10,11... | collective-permute-start | bytes 98312 | tf_op jit(solution)/shard_map/ppermute | solution.py:429
  28.7 4.0 %collective-permute-done.6 = bf16[64,256]{1,0:T(8,128)(2,1)S(1)} collective-permute-done((bf16[64,256]{1,0:T(8,128)(2,1)S(1)}, bf16[64,256]{1,0:T(8,128)(2,1)S(1)}, u32[]{:S(2)}, u32[]{:S(2)}) %collective-permute-start.6) | collective-permute-done | bytes 32800 | tf_op jit(solution)/shard_map/ppermute | solution.py:429
  32.7 0.7 %fusion.5 = (f32[32,512]{1,0:T(8,128)}, f32[32,512]{1,0:T(8,128)}) fusion(f32[64,512]{1,0:T(8,128)S(1)} %maximum_select_fusion), kind=kLoop, calls=%fused_computation.14 | loop fusion | bytes 262144 | tf_op jit(solution)/shard_map/slice | solution.py:433
  (6 shorter events, 0.1 us)
Async XLA Ops:
  1.8 10.7 %collective-permute-start = (bf16[32,128]{1,0:T(8,128)(2,1)S(1)}, bf16[32,128]{1,0:T(8,128)(2,1)S(1)}, u32[]{:S(2)}, u32[]{:S(2)}) collective-permute-start(bf16[32,128]{1,0:T(8,128)(2,1)S(1)} %get-tuple-element.16), channel_id=1, source_target_pairs={{0,2},{2,4},{4,6},{6,8},{8,10},{10,12},{12,14},{14,16},{16,18},{18... | collective-permute-start | bytes 24584 | tf_op jit(solution)/shard_map/ppermute | solution.py:330
  5.9 10.6 %collective-permute-start.3 = (bf16[280,128]{1,0:T(8,128)(2,1)S(1)}, bf16[280,128]{1,0:T(8,128)(2,1)S(1)}, u32[]{:S(2)}, u32[]{:S(2)}) collective-permute-start(bf16[280,128]{1,0:T(8,128)(2,1)S(1)} %pack.1.mine), channel_id=1, source_target_pairs={{0,1},{1,0},{2,3},{3,2},{4,5},{5,4},{6,7},{7,6},{8,9},{9,8},{10,11... | collective-permute-start | bytes 215048 | tf_op jit(solution)/shard_map/ppermute | solution.py:342
  12.7 5.2 %collective-permute-start.2 = (bf16[32,512]{1,0:T(8,128)(2,1)S(1)}, bf16[32,512]{1,0:T(8,128)(2,1)S(1)}, u32[]{:S(2)}, u32[]{:S(2)}) collective-permute-start(bf16[32,512]{1,0:T(8,128)(2,1)S(1)} %get-tuple-element.39.own), channel_id=1, source_target_pairs={{32,64},{64,32},{96,128},{128,96},{160,192},{192,160},{33,65},{65,... | collective-permute-start | bytes 98312 | tf_op jit(solution)/shard_map/ppermute | solution.py:360
  14.6 3.3 %collective-permute-start.1 = (bf16[32,512]{1,0:T(8,128)(2,1)S(1)}, bf16[32,512]{1,0:T(8,128)(2,1)S(1)}, u32[]{:S(2)}, u32[]{:S(2)}) collective-permute-start(bf16[32,512]{1,0:T(8,128)(2,1)S(1)} %get-tuple-element.39.own), channel_id=1, source_target_pairs={{0,32},{32,0},{64,96},{96,64},{128,160},{160,128},{192,224},{224,1... | collective-permute-start | bytes 98312 | tf_op jit(solution)/shard_map/ppermute | solution.py:359
  21.7 4.8 %collective-permute-start.4 = (f32[32,256]{1,0:T(8,128)S(1)}, f32[32,256]{1,0:T(8,128)S(1)}, u32[]{:S(2)}, u32[]{:S(2)}) collective-permute-start(f32[32,256]{1,0:T(8,128)S(1)} %get-tuple-element.27), channel_id=1, source_target_pairs={{0,32},{32,0},{64,96},{96,64},{128,160},{160,128},{192,224},{224,1... | collective-permute-start | bytes 98312 | tf_op jit(solution)/shard_map/ppermute | solution.py:415
  21.9 5.2 %collective-permute-start.5 = (f32[32,256]{1,0:T(8,128)S(1)}, f32[32,256]{1,0:T(8,128)S(1)}, u32[]{:S(2)}, u32[]{:S(2)}) collective-permute-start(f32[32,256]{1,0:T(8,128)S(1)} %get-tuple-element.28), channel_id=1, source_target_pairs={{32,64},{64,32},{96,128},{128,96},{160,192},{192,160},{33,65},{65,... | collective-permute-start | bytes 98312 | tf_op jit(solution)/shard_map/ppermute | solution.py:414
  27.2 5.5 %collective-permute-start.6 = (bf16[64,256]{1,0:T(8,128)(2,1)S(1)}, bf16[64,256]{1,0:T(8,128)(2,1)S(1)}, u32[]{:S(2)}, u32[]{:S(2)}) collective-permute-start(bf16[64,256]{1,0:T(8,128)(2,1)S(1)} %get-tuple-element.33), channel_id=1, source_target_pairs={{0,1},{1,0},{2,3},{3,2},{4,5},{5,4},{6,7},{7,6},{8,9},{9,8},{10,11... | collective-permute-start | bytes 98312 | tf_op jit(solution)/shard_map/ppermute | solution.py:429

commit v6 on v5

--- a/solution.py
+++ b/solution.py
@@ -233,8 +233,6 @@
     rows[17:49, :] = own[...].astype(F32)
     rows[49:66, :] = jnp.where(even, below, above)[0:17]
     rows[66:72, :] = jnp.zeros((6, 512), F32)
-    spread(rows, image, 0, 5)
-    spread(rows, image, 12, 17)
     spread_ends(rows, side, lines, ends)
     weight = wgt[...].reshape(3, 1, 16, 256)
     target = tgt[...].astype(F32)
@@ -250,15 +248,18 @@
     def respond(pixels, want):
         fields = jnp.dot(fwd[...], pixels, preferred_element_type=F32)
         fields = fields.reshape(3, BLOCK, 16, 256)
-        squares = weight * fields * fields
+        weighted = weight * fields
+        squares = weighted * fields
         intensity = jnp.sum((squares[0] + squares[1]) + squares[2], axis=1)
         resist = jax.nn.sigmoid(STEEP * (intensity - THRESHOLD))
-        slope = GAIN * (resist - want) * resist * (1.0 - resist)
+        slope = (2.0 * GAIN) * (resist - want) * resist * (1.0 - resist)
         slope = jnp.where(want > 1.5, 0.0, slope)
-        scaled = (2.0 * weight) * slope[None, :, None, :] * fields
+        scaled = weighted * slope[None, :, None, :]
         return resist, scaled.reshape(384, 256)
 
     resist_ends, scaled = respond(ends[...], jnp.concatenate(goal_ends, axis=1))
+    spread(rows, image, 0, 5)
+    spread(rows, image, 12, 17)
     for j in range(4):
         tile = scaled[:, 128 * (j // 2) : 128 * (j // 2) + 128]
         tile = pltpu.roll(tile, 120 - 64 * (j % 2), 1)

time: 33.6 us -> 33.5 us (level)
  no operation moved by 1% of the time
where the time goes in v6:
time: 33.5 us; the launch traced here: 33.4 us
  starting transfers between devices  18 us (54%)
  Pallas kernels  8.95 us (27%)
  waiting for transfers between devices  4.79 us (14%)
  between operations  0.76 us (2%)
  local copies, waits for them, and re-layouts  0.67 us (2%)
    ppermute x1, starting transfers between devices, per_device(): other = lax.ppermute(packed, 'kern', swap)  6.5 us
    ppermute x1, waiting for transfers between devices, per_device(): theirs = lax.ppermute(mine.astype(BF), 'kern', swap).astype(F32)  3.96 us
    ppermute x1, starting transfers between devices, per_device(): strip_in = lax.ppermute(strip, ('col', 'kern'), to_right + to_left)  3.83 us
    pallas_call x1, Pallas kernels, per_device(): pl.pallas_call(main_body, out_shape=(tile, tile, tile, jax.ShapeDtypeStru...  3.8 us
    ppermute x1, starting transfers between devices, per_device(): got_two = lax.ppermute(share_two, 'row', far)  2.29 us
    pallas_call x1, Pallas kernels, per_device(): pl.pallas_call(rest_body, out_shape=tile, in_specs=[VMEM] * 3, out_specs=...  2.26 us
    ppermute x1, starting transfers between devices, per_device(): two = lax.ppermute(own, 'row', far)  1.92 us
    ppermute x1, starting transfers between devices, per_device(): one = lax.ppermute(own, 'row', near)  1.68 us
  transfers between devices with their start and end apart: 7, of which 3 were waited for; matrix products, arithmetic and copies ran while one was open for 1% of the time, Pallas kernels for 12%

profile of v6, /device:TPU:10, one launch (start us, length us, event | category | flops | bytes accessed | tf_op | source)
XLA Modules:
  0.0 33.4 jit_solution(11840882160196136354)
XLA Ops:
  0.6 1.2 %start.1 = (bf16[32,128]{1,0:T(8,128)(2,1)S(1)}, f32[32,512]{1,0:T(8,128)S(1)}, bf16[32,512]{1,0:T(8,128)(2,1)S(1)}, bf16[32,512]{1,0:T(8,128)(2,1)S(1)}, bf16[1...) custom-call(s32[32,512]{1,0:T(8,128)} %levels.1, f32[32,512]{1,0:T(8,128)} %offset.1, s32[32,512]{1,0:T(8,128)} %bits.1, ...), custom_call_target="tpu_custom_call" | custom-call | tf_op jit(solution)/shard_map/start/pallas_call | solution.py:307
  1.8 3.8 %collective-permute-start = (bf16[32,128]{1,0:T(8,128)(2,1)S(1)}, bf16[32,128]{1,0:T(8,128)(2,1)S(1)}, u32[]{:S(2)}, u32[]{:S(2)}) collective-permute-start(bf16[32,128]{1,0:T(8,128)(2,1)S(1)} %get-tuple-element.16), channel_id=1, source_target_pairs={{0,2},{2,4},{4,6},{6,8},{8,10},{10,12},{12,14},{14,16},{16,18},{18... | collective-permute-start | bytes 24584 | tf_op jit(solution)/shard_map/ppermute | solution.py:331
  5.6 0.3 pack.1.mine
  5.9 6.5 %collective-permute-start.3 = (bf16[280,128]{1,0:T(8,128)(2,1)S(1)}, bf16[280,128]{1,0:T(8,128)(2,1)S(1)}, u32[]{:S(2)}, u32[]{:S(2)}) collective-permute-start(bf16[280,128]{1,0:T(8,128)(2,1)S(1)} %pack.1.mine), channel_id=1, source_target_pairs={{0,1},{1,0},{2,3},{3,2},{4,5},{5,4},{6,7},{7,6},{8,9},{9,8},{10,11... | collective-permute-start | bytes 215048 | tf_op jit(solution)/shard_map/ppermute | solution.py:343
  12.5 0.0 collective-permute-done
  12.5 0.1 slice_select_fusion
  12.6 0.1 fusion.1
  12.7 1.9 %collective-permute-start.2 = (bf16[32,512]{1,0:T(8,128)(2,1)S(1)}, bf16[32,512]{1,0:T(8,128)(2,1)S(1)}, u32[]{:S(2)}, u32[]{:S(2)}) collective-permute-start(bf16[32,512]{1,0:T(8,128)(2,1)S(1)} %get-tuple-element.39.own), channel_id=1, source_target_pairs={{32,64},{64,32},{96,128},{128,96},{160,192},{192,160},{33,65},{65,... | collective-permute-start | bytes 98312 | tf_op jit(solution)/shard_map/ppermute | solution.py:361
  14.6 1.7 %collective-permute-start.1 = (bf16[32,512]{1,0:T(8,128)(2,1)S(1)}, bf16[32,512]{1,0:T(8,128)(2,1)S(1)}, u32[]{:S(2)}, u32[]{:S(2)}) collective-permute-start(bf16[32,512]{1,0:T(8,128)(2,1)S(1)} %get-tuple-element.39.own), channel_id=1, source_target_pairs={{0,32},{32,0},{64,96},{96,64},{128,160},{160,128},{192,224},{224,1... | collective-permute-start | bytes 98312 | tf_op jit(solution)/shard_map/ppermute | solution.py:360
  16.3 0.3 own.1.image_in
  16.6 0.0 collective-permute-done.3.theirs
  16.6 1.1 %taps.1 = (bf16[384,1536]{1,0:T(8,128)(2,1)S(1)}, bf16[320,2304]{1,0:T(8,128)(2,1)S(1)}, f32[48,256]{1,0:T(8,128)S(1)}) custom-call(bf16[280,128]{1,0:T(8,128)(2,1)S(1)} %pack.1.mine, bf16[280,128]{1,0:T(8,128)(2,1)S(1)} %collective-permute-done.3.theirs), custom_call_target="tpu_custom_call" | custom-call | flops 400000000 | bytes 4000000 | tf_op jit(solution)/shard_map/taps/pallas_call | solution.py:372
  17.7 0.2 collective-permute-done.2.two
  17.9 0.0 collective-permute-done.1.one
  17.9 3.8 %fields.1 = (f32[32,256]{1,0:T(8,128)S(1)}, f32[32,256]{1,0:T(8,128)S(1)}, f32[32,256]{1,0:T(8,128)S(1)}, f32[8,256]{1,0:T(8,128)S(1)}, bf16[1536,384]{1,0:T(8,128)(2,1)S(1)}, /*index=5*/bf16[2448,256]{1,0:T(8,128)(2,1)S(1)}) custom-call(bf16[32,512]{1,0:T(8,128)(2,1)S(1)} %collective-permute-done.1.one, ...), custom_call_target="tpu_custom_call", output_to_operand_aliasing={{5}: (7, {})} | custom-call | flops 6000000000 | bytes 6000000 | tf_op jit(solution)/shard_map/fields/pallas_call | solution.py:390
  21.7 0.2 collective-permute-start.4
  21.9 2.3 %collective-permute-start.5 = (f32[32,256]{1,0:T(8,128)S(1)}, f32[32,256]{1,0:T(8,128)S(1)}, u32[]{:S(2)}, u32[]{:S(2)}) collective-permute-start(f32[32,256]{1,0:T(8,128)S(1)} %get-tuple-element.28), channel_id=1, source_target_pairs={{32,64},{64,32},{96,128},{128,96},{160,192},{192,160},{33,65},{65,... | collective-permute-start | bytes 98312 | tf_op jit(solution)/shard_map/ppermute | solution.py:415
  24.2 2.3 %inner.1 = f32[32,256]{1,0:T(8,128)S(1)} custom-call(bf16[320,2304]{1,0:T(8,128)(2,1)S(1)} %get-tuple-element.23.adj, bf16[1536,384]{1,0:T(8,128)(2,1)S(1)} %get-tuple-element.25.charge, f32[8,256]{1,0:T(8,128)S(1)} %get-tuple-element.26.some), custom_call_target="tpu_custom_call" | custom-call | flops 2000000000 | bytes 3000000 | tf_op jit(solution)/shard_map/inner/pallas_call | solution.py:417
  26.5 0.0 collective-permute-done.4
  26.5 0.6 %collective-permute-done.5 = f32[32,256]{1,0:T(8,128)S(1)} collective-permute-done((f32[32,256]{1,0:T(8,128)S(1)}, f32[32,256]{1,0:T(8,128)S(1)}, u32[]{:S(2)}, u32[]{:S(2)}) %collective-permute-start.5) | collective-permute-done | bytes 32800 | tf_op jit(solution)/shard_map/ppermute | solution.py:415
  27.2 1.5 %collective-permute-start.6 = (bf16[64,256]{1,0:T(8,128)(2,1)S(1)}, bf16[64,256]{1,0:T(8,128)(2,1)S(1)}, u32[]{:S(2)}, u32[]{:S(2)}) collective-permute-start(bf16[64,256]{1,0:T(8,128)(2,1)S(1)} %get-tuple-element.33), channel_id=1, source_target_pairs={{0,1},{1,0},{2,3},{3,2},{4,5},{5,4},{6,7},{7,6},{8,9},{9,8},{10,11... | collective-permute-start | bytes 98312 | tf_op jit(solution)/shard_map/ppermute | solution.py:430
  28.7 4.0 %collective-permute-done.6 = bf16[64,256]{1,0:T(8,128)(2,1)S(1)} collective-permute-done((bf16[64,256]{1,0:T(8,128)(2,1)S(1)}, bf16[64,256]{1,0:T(8,128)(2,1)S(1)}, u32[]{:S(2)}, u32[]{:S(2)}) %collective-permute-start.6) | collective-permute-done | bytes 32800 | tf_op jit(solution)/shard_map/ppermute | solution.py:430
  32.7 0.7 %fusion.5 = (f32[32,512]{1,0:T(8,128)}, f32[32,512]{1,0:T(8,128)}) fusion(f32[64,512]{1,0:T(8,128)S(1)} %maximum_select_fusion), kind=kLoop, calls=%fused_computation.14 | loop fusion | bytes 262144 | tf_op jit(solution)/shard_map/slice | solution.py:434
  (6 shorter events, 0.1 us)
Async XLA Ops:
  1.8 10.7 %collective-permute-start = (bf16[32,128]{1,0:T(8,128)(2,1)S(1)}, bf16[32,128]{1,0:T(8,128)(2,1)S(1)}, u32[]{:S(2)}, u32[]{:S(2)}) collective-permute-start(bf16[32,128]{1,0:T(8,128)(2,1)S(1)} %get-tuple-element.16), channel_id=1, source_target_pairs={{0,2},{2,4},{4,6},{6,8},{8,10},{10,12},{12,14},{14,16},{16,18},{18... | collective-permute-start | bytes 24584 | tf_op jit(solution)/shard_map/ppermute | solution.py:331
  5.9 10.6 %collective-permute-start.3 = (bf16[280,128]{1,0:T(8,128)(2,1)S(1)}, bf16[280,128]{1,0:T(8,128)(2,1)S(1)}, u32[]{:S(2)}, u32[]{:S(2)}) collective-permute-start(bf16[280,128]{1,0:T(8,128)(2,1)S(1)} %pack.1.mine), channel_id=1, source_target_pairs={{0,1},{1,0},{2,3},{3,2},{4,5},{5,4},{6,7},{7,6},{8,9},{9,8},{10,11... | collective-permute-start | bytes 215048 | tf_op jit(solution)/shard_map/ppermute | solution.py:343
  12.7 5.2 %collective-permute-start.2 = (bf16[32,512]{1,0:T(8,128)(2,1)S(1)}, bf16[32,512]{1,0:T(8,128)(2,1)S(1)}, u32[]{:S(2)}, u32[]{:S(2)}) collective-permute-start(bf16[32,512]{1,0:T(8,128)(2,1)S(1)} %get-tuple-element.39.own), channel_id=1, source_target_pairs={{32,64},{64,32},{96,128},{128,96},{160,192},{192,160},{33,65},{65,... | collective-permute-start | bytes 98312 | tf_op jit(solution)/shard_map/ppermute | solution.py:361
  14.6 3.3 %collective-permute-start.1 = (bf16[32,512]{1,0:T(8,128)(2,1)S(1)}, bf16[32,512]{1,0:T(8,128)(2,1)S(1)}, u32[]{:S(2)}, u32[]{:S(2)}) collective-permute-start(bf16[32,512]{1,0:T(8,128)(2,1)S(1)} %get-tuple-element.39.own), channel_id=1, source_target_pairs={{0,32},{32,0},{64,96},{96,64},{128,160},{160,128},{192,224},{224,1... | collective-permute-start | bytes 98312 | tf_op jit(solution)/shard_map/ppermute | solution.py:360
  21.7 4.8 %collective-permute-start.4 = (f32[32,256]{1,0:T(8,128)S(1)}, f32[32,256]{1,0:T(8,128)S(1)}, u32[]{:S(2)}, u32[]{:S(2)}) collective-permute-start(f32[32,256]{1,0:T(8,128)S(1)} %get-tuple-element.27), channel_id=1, source_target_pairs={{0,32},{32,0},{64,96},{96,64},{128,160},{160,128},{192,224},{224,1... | collective-permute-start | bytes 98312 | tf_op jit(solution)/shard_map/ppermute | solution.py:416
  21.9 5.2 %collective-permute-start.5 = (f32[32,256]{1,0:T(8,128)S(1)}, f32[32,256]{1,0:T(8,128)S(1)}, u32[]{:S(2)}, u32[]{:S(2)}) collective-permute-start(f32[32,256]{1,0:T(8,128)S(1)} %get-tuple-element.28), channel_id=1, source_target_pairs={{32,64},{64,32},{96,128},{128,96},{160,192},{192,160},{33,65},{65,... | collective-permute-start | bytes 98312 | tf_op jit(solution)/shard_map/ppermute | solution.py:415
  27.2 5.5 %collective-permute-start.6 = (bf16[64,256]{1,0:T(8,128)(2,1)S(1)}, bf16[64,256]{1,0:T(8,128)(2,1)S(1)}, u32[]{:S(2)}, u32[]{:S(2)}) collective-permute-start(bf16[64,256]{1,0:T(8,128)(2,1)S(1)} %get-tuple-element.33), channel_id=1, source_target_pairs={{0,1},{1,0},{2,3},{3,2},{4,5},{5,4},{6,7},{7,6},{8,9},{9,8},{10,11... | collective-permute-start | bytes 98312 | tf_op jit(solution)/shard_map/ppermute | solution.py:430

commit v7 on v5

--- a/solution.py
+++ b/solution.py
@@ -283,8 +283,8 @@
                 some_out[...] = jnp.broadcast_to(fold(part, i), (8, 256))
             else:
                 dn_out[x - ROWS : x - ROWS + 1, :] = fold(part, i)
-    one_out[...] = jnp.where(even, dn_out[...], up_out[...])
-    two_out[...] = jnp.where(even, up_out[...], dn_out[...])
+    one_out[...] = jnp.where(even, dn_out[...], up_out[...]).astype(BF)
+    two_out[...] = jnp.where(even, up_out[...], dn_out[...]).astype(BF)
 
 
 def rest_body(adj, charge, some, mid_out):
@@ -390,8 +390,8 @@
         main_body,
         out_shape=(
             tile,
-            tile,
-            tile,
+            jax.ShapeDtypeStruct((ROWS, 256), BF),
+            jax.ShapeDtypeStruct((ROWS, 256), BF),
             jax.ShapeDtypeStruct((8, 256), F32),
             jax.ShapeDtypeStruct((1536, WIDE), BF),
             jax.ShapeDtypeStruct((IMAGE, 256), BF),
@@ -423,7 +423,7 @@
         name="inner",
     )(adj, charge, some)
     half = jnp.where(left, mask_full[:, :256], mask_full[:, 256:])
-    gradient = (middle_rows + got_one + got_two) * half * (1.0 - half)
+    gradient = (middle_rows + got_one.astype(F32) + got_two.astype(F32)) * half * (1.0 - half)
     mine = jnp.concatenate([resist, gradient], axis=0)
     mine = lax.reduce_precision(mine, 8, 7)
     theirs = lax.ppermute(mine.astype(BF), "kern", swap).astype(F32)

time: 33.6 us -> 33.4 us (level)
  no operation moved by 1% of the time
where the time goes in v7:
time: 33.4 us; the launch traced here: 33.3 us
  starting transfers between devices  18 us (54%)
  Pallas kernels  8.97 us (27%)
  waiting for transfers between devices  4.67 us (14%)
  between operations  0.76 us (2%)
  local copies, waits for them, and re-layouts  0.67 us (2%)
    ppermute x1, starting transfers between devices, per_device(): other = lax.ppermute(packed, 'kern', swap)  6.5 us
    ppermute x1, waiting for transfers between devices, per_device(): theirs = lax.ppermute(mine.astype(BF), 'kern', swap).astype(F32)  4.01 us
    ppermute x1, starting transfers between devices, per_device(): strip_in = lax.ppermute(strip, ('col', 'kern'), to_right + to_left)  3.83 us
    pallas_call x1, Pallas kernels, per_device(): pl.pallas_call(main_body, out_shape=(tile, jax.ShapeDtypeStruct((ROWS, 25...  3.81 us
    ppermute x1, starting transfers between devices, per_device(): got_two = lax.ppermute(share_two, 'row', far)  2.28 us
    pallas_call x1, Pallas kernels, per_device(): pl.pallas_call(rest_body, out_shape=tile, in_specs=[VMEM] * 3, out_specs=...  2.26 us
    ppermute x1, starting transfers between devices, per_device(): two = lax.ppermute(own, 'row', far)  1.92 us
    ppermute x1, starting transfers between devices, per_device(): one = lax.ppermute(own, 'row', near)  1.68 us
  transfers between devices with their start and end apart: 7, of which 3 were waited for; matrix products, arithmetic and copies ran while one was open for 1% of the time, Pallas kernels for 12%

profile of v7, /device:TPU:10, one launch (start us, length us, event | category | flops | bytes accessed | tf_op | source)
XLA Modules:
  0.0 33.3 jit_solution(5914958108128930210)
XLA Ops:
  0.6 1.2 %start.1 = (bf16[32,128]{1,0:T(8,128)(2,1)S(1)}, f32[32,512]{1,0:T(8,128)S(1)}, bf16[32,512]{1,0:T(8,128)(2,1)S(1)}, bf16[32,512]{1,0:T(8,128)(2,1)S(1)}, bf16[1...) custom-call(s32[32,512]{1,0:T(8,128)} %levels.1, f32[32,512]{1,0:T(8,128)} %offset.1, s32[32,512]{1,0:T(8,128)} %bits.1, ...), custom_call_target="tpu_custom_call" | custom-call | tf_op jit(solution)/shard_map/start/pallas_call | solution.py:306
  1.8 3.8 %collective-permute-start = (bf16[32,128]{1,0:T(8,128)(2,1)S(1)}, bf16[32,128]{1,0:T(8,128)(2,1)S(1)}, u32[]{:S(2)}, u32[]{:S(2)}) collective-permute-start(bf16[32,128]{1,0:T(8,128)(2,1)S(1)} %get-tuple-element.16), channel_id=1, source_target_pairs={{0,2},{2,4},{4,6},{6,8},{8,10},{10,12},{12,14},{14,16},{16,18},{18... | collective-permute-start | bytes 24584 | tf_op jit(solution)/shard_map/ppermute | solution.py:330
  5.6 0.3 pack.1.mine
  5.9 6.5 %collective-permute-start.3 = (bf16[280,128]{1,0:T(8,128)(2,1)S(1)}, bf16[280,128]{1,0:T(8,128)(2,1)S(1)}, u32[]{:S(2)}, u32[]{:S(2)}) collective-permute-start(bf16[280,128]{1,0:T(8,128)(2,1)S(1)} %pack.1.mine), channel_id=1, source_target_pairs={{0,1},{1,0},{2,3},{3,2},{4,5},{5,4},{6,7},{7,6},{8,9},{9,8},{10,11... | collective-permute-start | bytes 215048 | tf_op jit(solution)/shard_map/ppermute | solution.py:342
  12.5 0.0 collective-permute-done
  12.5 0.1 slice_select_fusion
  12.6 0.1 fusion.1
  12.7 1.9 %collective-permute-start.2 = (bf16[32,512]{1,0:T(8,128)(2,1)S(1)}, bf16[32,512]{1,0:T(8,128)(2,1)S(1)}, u32[]{:S(2)}, u32[]{:S(2)}) collective-permute-start(bf16[32,512]{1,0:T(8,128)(2,1)S(1)} %get-tuple-element.39.own), channel_id=1, source_target_pairs={{32,64},{64,32},{96,128},{128,96},{160,192},{192,160},{33,65},{65,... | collective-permute-start | bytes 98312 | tf_op jit(solution)/shard_map/ppermute | solution.py:360
  14.6 1.7 %collective-permute-start.1 = (bf16[32,512]{1,0:T(8,128)(2,1)S(1)}, bf16[32,512]{1,0:T(8,128)(2,1)S(1)}, u32[]{:S(2)}, u32[]{:S(2)}) collective-permute-start(bf16[32,512]{1,0:T(8,128)(2,1)S(1)} %get-tuple-element.39.own), channel_id=1, source_target_pairs={{0,32},{32,0},{64,96},{96,64},{128,160},{160,128},{192,224},{224,1... | collective-permute-start | bytes 98312 | tf_op jit(solution)/shard_map/ppermute | solution.py:359
  16.3 0.3 own.1.image_in
  16.6 0.0 collective-permute-done.3.theirs
  16.6 1.1 %taps.1 = (bf16[384,1536]{1,0:T(8,128)(2,1)S(1)}, bf16[320,2304]{1,0:T(8,128)(2,1)S(1)}, f32[48,256]{1,0:T(8,128)S(1)}) custom-call(bf16[280,128]{1,0:T(8,128)(2,1)S(1)} %pack.1.mine, bf16[280,128]{1,0:T(8,128)(2,1)S(1)} %collective-permute-done.3.theirs), custom_call_target="tpu_custom_call" | custom-call | flops 400000000 | bytes 4000000 | tf_op jit(solution)/shard_map/taps/pallas_call | solution.py:371
  17.7 0.2 collective-permute-done.2.two
  17.9 0.0 collective-permute-done.1.one
  17.9 3.8 %fields.1 = (f32[32,256]{1,0:T(8,128)S(1)}, bf16[32,256]{1,0:T(8,128)(2,1)S(1)}, bf16[32,256]{1,0:T(8,128)(2,1)S(1)}, f32[8,256]{1,0:T(8,128)S(1)}, bf16[1536,38...) custom-call(bf16[32,512]{1,0:T(8,128)(2,1)S(1)} %collective-permute-done.1.one, ...), custom_call_target="tpu_custom_call", output_to_operand_aliasing={{5}: (7, {})} | custom-call | flops 6000000000 | bytes 6000000 | tf_op jit(solution)/shard_map/fields/pallas_call | solution.py:389
  21.7 0.2 collective-permute-start.4
  21.9 2.3 %collective-permute-start.5 = (bf16[32,256]{1,0:T(8,128)(2,1)S(1)}, bf16[32,256]{1,0:T(8,128)(2,1)S(1)}, u32[]{:S(2)}, u32[]{:S(2)}) collective-permute-start(bf16[32,256]{1,0:T(8,128)(2,1)S(1)} %get-tuple-element.28), channel_id=1, source_target_pairs={{32,64},{64,32},{96,128},{128,96},{160,192},{192,160},{33,65},{65,... | collective-permute-start | bytes 49160 | tf_op jit(solution)/shard_map/ppermute | solution.py:414
  24.2 2.3 %inner.1 = f32[32,256]{1,0:T(8,128)S(1)} custom-call(bf16[320,2304]{1,0:T(8,128)(2,1)S(1)} %get-tuple-element.23.adj, bf16[1536,384]{1,0:T(8,128)(2,1)S(1)} %get-tuple-element.25.charge, f32[8,256]{1,0:T(8,128)S(1)} %get-tuple-element.26.some), custom_call_target="tpu_custom_call" | custom-call | flops 2000000000 | bytes 3000000 | tf_op jit(solution)/shard_map/inner/pallas_call | solution.py:416
  26.5 0.0 collective-permute-done.4
  26.5 0.5 %collective-permute-done.5 = bf16[32,256]{1,0:T(8,128)(2,1)S(1)} collective-permute-done((bf16[32,256]{1,0:T(8,128)(2,1)S(1)}, bf16[32,256]{1,0:T(8,128)(2,1)S(1)}, u32[]{:S(2)}, u32[]{:S(2)}) %collective-permute-start.5) | collective-permute-done | bytes 16416 | tf_op jit(solution)/shard_map/ppermute | solution.py:414
  27.0 1.5 %collective-permute-start.6 = (bf16[64,256]{1,0:T(8,128)(2,1)S(1)}, bf16[64,256]{1,0:T(8,128)(2,1)S(1)}, u32[]{:S(2)}, u32[]{:S(2)}) collective-permute-start(bf16[64,256]{1,0:T(8,128)(2,1)S(1)} %get-tuple-element.33), channel_id=1, source_target_pairs={{0,1},{1,0},{2,3},{3,2},{4,5},{5,4},{6,7},{7,6},{8,9},{9,8},{10,11... | collective-permute-start | bytes 98312 | tf_op jit(solution)/shard_map/ppermute | solution.py:429
  28.6 4.0 %collective-permute-done.6 = bf16[64,256]{1,0:T(8,128)(2,1)S(1)} collective-permute-done((bf16[64,256]{1,0:T(8,128)(2,1)S(1)}, bf16[64,256]{1,0:T(8,128)(2,1)S(1)}, u32[]{:S(2)}, u32[]{:S(2)}) %collective-permute-start.6) | collective-permute-done | bytes 32800 | tf_op jit(solution)/shard_map/ppermute | solution.py:429
  32.6 0.7 %fusion.5 = (f32[32,512]{1,0:T(8,128)}, f32[32,512]{1,0:T(8,128)}) fusion(f32[64,512]{1,0:T(8,128)S(1)} %maximum_select_fusion), kind=kLoop, calls=%fused_computation.14 | loop fusion | bytes 262144 | tf_op jit(solution)/shard_map/slice | solution.py:433
  (6 shorter events, 0.1 us)
Async XLA Ops:
  1.8 10.7 %collective-permute-start = (bf16[32,128]{1,0:T(8,128)(2,1)S(1)}, bf16[32,128]{1,0:T(8,128)(2,1)S(1)}, u32[]{:S(2)}, u32[]{:S(2)}) collective-permute-start(bf16[32,128]{1,0:T(8,128)(2,1)S(1)} %get-tuple-element.16), channel_id=1, source_target_pairs={{0,2},{2,4},{4,6},{6,8},{8,10},{10,12},{12,14},{14,16},{16,18},{18... | collective-permute-start | bytes 24584 | tf_op jit(solution)/shard_map/ppermute | solution.py:330
  5.9 10.6 %collective-permute-start.3 = (bf16[280,128]{1,0:T(8,128)(2,1)S(1)}, bf16[280,128]{1,0:T(8,128)(2,1)S(1)}, u32[]{:S(2)}, u32[]{:S(2)}) collective-permute-start(bf16[280,128]{1,0:T(8,128)(2,1)S(1)} %pack.1.mine), channel_id=1, source_target_pairs={{0,1},{1,0},{2,3},{3,2},{4,5},{5,4},{6,7},{7,6},{8,9},{9,8},{10,11... | collective-permute-start | bytes 215048 | tf_op jit(solution)/shard_map/ppermute | solution.py:342
  12.7 5.2 %collective-permute-start.2 = (bf16[32,512]{1,0:T(8,128)(2,1)S(1)}, bf16[32,512]{1,0:T(8,128)(2,1)S(1)}, u32[]{:S(2)}, u32[]{:S(2)}) collective-permute-start(bf16[32,512]{1,0:T(8,128)(2,1)S(1)} %get-tuple-element.39.own), channel_id=1, source_target_pairs={{32,64},{64,32},{96,128},{128,96},{160,192},{192,160},{33,65},{65,... | collective-permute-start | bytes 98312 | tf_op jit(solution)/shard_map/ppermute | solution.py:360
  14.6 3.3 %collective-permute-start.1 = (bf16[32,512]{1,0:T(8,128)(2,1)S(1)}, bf16[32,512]{1,0:T(8,128)(2,1)S(1)}, u32[]{:S(2)}, u32[]{:S(2)}) collective-permute-start(bf16[32,512]{1,0:T(8,128)(2,1)S(1)} %get-tuple-element.39.own), channel_id=1, source_target_pairs={{0,32},{32,0},{64,96},{96,64},{128,160},{160,128},{192,224},{224,1... | collective-permute-start | bytes 98312 | tf_op jit(solution)/shard_map/ppermute | solution.py:359
  21.7 4.8 %collective-permute-start.4 = (bf16[32,256]{1,0:T(8,128)(2,1)S(1)}, bf16[32,256]{1,0:T(8,128)(2,1)S(1)}, u32[]{:S(2)}, u32[]{:S(2)}) collective-permute-start(bf16[32,256]{1,0:T(8,128)(2,1)S(1)} %get-tuple-element.27), channel_id=1, source_target_pairs={{0,32},{32,0},{64,96},{96,64},{128,160},{160,128},{192,224},{224,1... | collective-permute-start | bytes 49160 | tf_op jit(solution)/shard_map/ppermute | solution.py:415
  21.9 5.0 %collective-permute-start.5 = (bf16[32,256]{1,0:T(8,128)(2,1)S(1)}, bf16[32,256]{1,0:T(8,128)(2,1)S(1)}, u32[]{:S(2)}, u32[]{:S(2)}) collective-permute-start(bf16[32,256]{1,0:T(8,128)(2,1)S(1)} %get-tuple-element.28), channel_id=1, source_target_pairs={{32,64},{64,32},{96,128},{128,96},{160,192},{192,160},{33,65},{65,... | collective-permute-start | bytes 49160 | tf_op jit(solution)/shard_map/ppermute | solution.py:414
  27.0 5.6 %collective-permute-start.6 = (bf16[64,256]{1,0:T(8,128)(2,1)S(1)}, bf16[64,256]{1,0:T(8,128)(2,1)S(1)}, u32[]{:S(2)}, u32[]{:S(2)}) collective-permute-start(bf16[64,256]{1,0:T(8,128)(2,1)S(1)} %get-tuple-element.33), channel_id=1, source_target_pairs={{0,1},{1,0},{2,3},{3,2},{4,5},{5,4},{6,7},{7,6},{8,9},{9,8},{10,11... | collective-permute-start | bytes 98312 | tf_op jit(solution)/shard_map/ppermute | solution.py:429
